TPU v7x, 32 devices: a whole 2x2x4 slice. The times are simulated.
32 devices in a mesh: req: 8 (over z, y), tp: 4 (over x, core).
Axes of the slice: x: 2, y: 2, z: 4, core: 2. Of those that a mesh axis runs over, the one named last changes fastest.
Arguments:
- residual: bfloat16 [256, 2048], P('req'), may hold values from -6 to 6
- cache_lengths: int32 [256], P('req'), may hold values from 4 to 4096, as said below
- input_gain: float32 [2048], replicated, may hold values from 0.1 to 1.9
- inner_weight: bfloat16 [2048, 2, 1536], P(None, None, 'tp'), may hold values from -0.125 to 0.125
- step_weight: bfloat16 [2048, 24], P(None, 'tp'), may hold values from -0.125 to 0.125
- step_bias: float32 [24], P('tp'), may hold values from -4 to -1
- decay_log: float32 [24], P('tp'), may hold values from 0 to 2.77
- skip_gain: float32 [24], P('tp'), may hold values from 0.5 to 2
- conv_weight: bfloat16 [4, 1536], P(None, 'tp'), may hold values from -3 to 3
- conv_state: bfloat16 [256, 3, 1536], P('req', None, 'tp'), may hold values from -6 to 6
- coupling_weight: bfloat16 [2048, 512], P(None, 'tp'), may hold values from -0.125 to 0.125
- coupling_conv: bfloat16 [4, 512], P(None, 'tp'), may hold values from -3 to 3
- coupling_state: bfloat16 [256, 3, 512], P('req', None, 'tp'), may hold values from -6 to 6
- scan_state: bfloat16 [256, 24, 64, 256], P('req', 'tp'), may hold values from -30 to 30
- mixer_gain: float32 [1536], P('tp'), may hold values from 0.1 to 1.9
- attention_weight: bfloat16 [2048, 1536], P(None, 'tp'), may hold values from -0.125 to 0.125
- sink_cache: bfloat16 [256, 4, 512], P('req'), may hold values from -2000 to 2000
- window_cache: bfloat16 [256, 1024, 512], P('req', 'tp'), may hold values from -9 to 9
- mamba_out: bfloat16 [1536, 2048], P('tp'), may hold values from -0.15625 to 0.15625
- attention_out: bfloat16 [1024, 2048], P('tp'), may hold values from -0.5 to 0.5
- final_gain: float32 [2048], replicated, may hold values from 0.1 to 1.9
- output_head: bfloat16 [2048, 65536], P(None, ('req', 'tp')), may hold values from -0.375 to 0.375
Outputs:
- new_residual: bfloat16 [256, 2048], P('req', 'tp')
- logits: float32 [256, 65536], P(('req', 'tp'))
- new_scan_state: bfloat16 [256, 24, 64, 256], P('req', 'tp')
- new_conv_state: bfloat16 [256, 3, 1536], P('req', None, 'tp')
- new_coupling_state: bfloat16 [256, 3, 512], P('req', None, 'tp')
- new_key_value: bfloat16 [256, 512], P('req')
Inputs may be any that keep to these rules, and one draw needn't show every extreme that they name: `cache_lengths`: A request's cache holds positions 0 to its length - 1; the new token stands at the position equal to the length. Some request has length exactly 4096.
All inputs are finite; a program needn't handle non-finite values.
Results may differ from a plain program's by a relative error of at most 0.02.
Values may be sent and summed in bfloat16 or wider, within the bound.
A program may use at most 128 MiB of HBM per device.

v0:
```python
import jax
import jax.numpy as jnp
from jax import lax
from jax.sharding import PartitionSpec as P

MH = 24
MP = 64
NS = 256
QH = 8
KVH = 2
HD = 128
WIN = 1024
SINK = 4


EPSILON = 1e-05
NEG_BIG = -1e30


def combined_all(array, axis, combine):
    everything = jax.tree.map(
        lambda part, kind: lax.all_gather(part.astype(kind), axis),
        array,
        (jnp.bfloat16, jnp.bfloat16, jnp.bfloat16),
    )

    def take(k):
        return jax.tree.map(lambda part, own: part[k].astype(own.dtype), everything, array)

    return lax.fori_loop(
        1, lax.axis_size(axis), lambda k, so_far: combine(so_far, take(k)), take(0)
    )


def norm_rows(values, gain):
    widened = values.astype(jnp.float32)
    mean_sq = jnp.mean(widened * widened, axis=-1, keepdims=True)
    return (widened * lax.rsqrt(mean_sq + EPSILON) * gain).astype(jnp.bfloat16)


def conv_apply(old_state, fresh_row, taps):
    window = jnp.concatenate([old_state, fresh_row[:, None, :]], axis=1)
    mixed_rows = jnp.einsum("rkc,kc->rc", window, taps, preferred_element_type=jnp.float32)
    return (jax.nn.silu(mixed_rows), window[:, 1:, :])


def merge_parts(first_part, second_part):
    first_peak, first_total, first_sum = first_part
    second_peak, second_total, second_sum = second_part
    row_peak = jnp.maximum(first_peak, second_peak)
    first_scale = jnp.exp(first_peak - row_peak)
    second_scale = jnp.exp(second_peak - row_peak)
    return (
        row_peak,
        first_total * first_scale + second_total * second_scale,
        first_sum * first_scale[..., None] + second_sum * second_scale[..., None],
    )


def attend_part(queries, key_rows, value_rows, valid_mask):
    scores = jnp.einsum(
        "rkgd,rskd->rkgs", queries, key_rows, preferred_element_type=jnp.float32
    ) * HD ** (-0.5)
    masked = jnp.where(valid_mask, scores, NEG_BIG)
    row_peak = jnp.max(masked, axis=-1)
    weights = jnp.where(valid_mask, jnp.exp(masked - row_peak[..., None]), 0.0)
    totals = jnp.sum(weights, axis=-1)
    summed = jnp.einsum(
        "rkgs,rskd->rkgd",
        weights.astype(jnp.bfloat16),
        value_rows,
        preferred_element_type=jnp.float32,
    )
    return (row_peak, totals, summed)


def body(
    residual,
    cache_lengths,
    input_gain,
    inner_weight,
    step_weight,
    step_bias,
    decay_log,
    skip_gain,
    conv_weight,
    conv_state,
    coupling_weight,
    coupling_conv,
    coupling_state,
    scan_state,
    mixer_gain,
    attention_weight,
    sink_cache,
    window_cache,
    mamba_out,
    attention_out,
    final_gain,
    output_head,
):
    row_count = residual.shape[0]
    tp_size = lax.axis_size("tp")
    tp_index = lax.axis_index("tp")
    local_heads = scan_state.shape[1]
    local_units = inner_weight.shape[2]
    half_width = KVH * HD
    group_size = QH // KVH
    normed = norm_rows(residual, input_gain)
    projected = jnp.einsum(
        "rd,dtc->rtc", normed, inner_weight, preferred_element_type=jnp.float32
    ).astype(jnp.bfloat16)
    gate_rows = lax.optimization_barrier(projected[:, 0, :])
    x_rows, new_conv_state = conv_apply(conv_state, projected[:, 1, :], conv_weight)
    step_rows = lax.optimization_barrier(
        jnp.dot(normed, step_weight, preferred_element_type=jnp.float32).astype(jnp.bfloat16)
    )
    step_size = jax.nn.softplus(step_rows.astype(jnp.float32) + step_bias)
    decay_rate = jnp.exp(-step_size * jnp.exp(decay_log))
    coupling_pre = jnp.dot(normed, coupling_weight, preferred_element_type=jnp.float32).astype(
        jnp.bfloat16
    )
    coupling_rows, new_coupling_state = conv_apply(coupling_state, coupling_pre, coupling_conv)
    qkv_local = jnp.dot(normed, attention_weight, preferred_element_type=jnp.float32).astype(
        jnp.bfloat16
    )
    qkv_rows, coupling_all = (
        lax.all_gather(qkv_local, "tp", axis=1, tiled=True),
        lax.all_gather(coupling_rows.astype(jnp.bfloat16), "tp", axis=1, tiled=True),
    )
    input_vec = coupling_all[:, :NS].astype(jnp.float32)
    output_vec = coupling_all[:, NS:].astype(jnp.float32)
    x_heads = x_rows.reshape(row_count, local_heads, MP)
    updated = (
        decay_rate[:, :, None, None] * scan_state.astype(jnp.float32)
        + (step_size[:, :, None] * x_heads)[:, :, :, None] * input_vec[:, None, None, :]
    )
    readout = (
        jnp.einsum("rhpn,rn->rhp", updated, output_vec, precision=lax.Precision.HIGHEST)
        + skip_gain[None, :, None] * x_heads
    )
    new_scan_state = updated.astype(jnp.bfloat16)
    gated_rows = readout.reshape(row_count, local_units) * jax.nn.silu(
        gate_rows.astype(jnp.float32)
    )
    square_total = lax.psum(jnp.sum(gated_rows * gated_rows, axis=1), "tp")
    mamba_rows = (
        gated_rows * lax.rsqrt(square_total / (MH * MP) + EPSILON)[:, None] * mixer_gain
    ).astype(jnp.bfloat16)
    queries = qkv_rows[:, : QH * HD].reshape(row_count, KVH, group_size, HD)
    fresh_keys = qkv_rows[:, QH * HD : QH * HD + half_width].reshape(row_count, 1, KVH, HD)
    fresh_values = qkv_rows[:, QH * HD + half_width :].reshape(row_count, 1, KVH, HD)
    new_key_value = qkv_rows[:, QH * HD :]
    is_lead = tp_index == 0
    sink_keys = sink_cache[:, :, :half_width].reshape(row_count, SINK, KVH, HD)
    sink_values = sink_cache[:, :, half_width:].reshape(row_count, SINK, KVH, HD)
    sink_part = attend_part(
        queries, sink_keys, sink_values, jnp.broadcast_to(is_lead, (row_count, 1, 1, SINK))
    )
    fresh_part = attend_part(
        queries, fresh_keys, fresh_values, jnp.broadcast_to(is_lead, (row_count, 1, 1, 1))
    )
    window_slots = window_cache.shape[1]
    slot_offset = tp_index * window_slots
    length_column = cache_lengths[:, None]
    cycle_keys = window_cache[:, :, :half_width].reshape(row_count, window_slots, KVH, HD)
    cycle_values = window_cache[:, :, half_width:].reshape(row_count, window_slots, KVH, HD)
    slot_index = slot_offset + jnp.arange(window_slots, dtype=jnp.int32)
    back_steps = (length_column - 1 - slot_index[None, :]) % WIN
    position = length_column - 1 - back_steps
    live_mask = ((position >= SINK) & (back_steps != WIN - 1))[:, None, None, :]
    cycle_part = attend_part(queries, cycle_keys, cycle_values, live_mask)
    local_peak, local_total, local_sum = merge_parts(merge_parts(sink_part, fresh_part), cycle_part)
    row_peak, totals, summed = combined_all((local_peak, local_total, local_sum), "tp", merge_parts)
    attended = (summed / totals[..., None]).reshape(row_count, QH * HD).astype(jnp.bfloat16)
    head_columns = QH // tp_size * HD
    own_heads = lax.dynamic_slice_in_dim(attended, tp_index * head_columns, head_columns, 1)
    mixed_rows = jnp.dot(mamba_rows, mamba_out, preferred_element_type=jnp.float32) + jnp.dot(
        own_heads, attention_out, preferred_element_type=jnp.float32
    )
    share_width = residual.shape[1] // tp_size
    mixed_total = lax.psum(mixed_rows.astype(jnp.bfloat16), "tp").astype(jnp.float32)
    new_full = (residual.astype(jnp.float32) + mixed_total).astype(jnp.bfloat16)
    new_residual = lax.dynamic_slice_in_dim(new_full, tp_index * share_width, share_width, 1)
    final_rows = norm_rows(new_full, final_gain)
    vocab_logits = jnp.dot(
        lax.all_gather(final_rows, "req", axis=0, tiled=True),
        output_head,
        preferred_element_type=jnp.float32,
    )
    logits = lax.all_to_all(
        vocab_logits.astype(jnp.bfloat16), ("req", "tp"), split_axis=0, concat_axis=1, tiled=True
    ).astype(vocab_logits.dtype)
    return (new_residual, logits, new_scan_state, new_conv_state, new_coupling_state, new_key_value)


def solution(mesh):
    return jax.shard_map(
        body,
        mesh=mesh,
        in_specs=(
            P("req", None),
            P("req"),
            P(),
            P(None, None, "tp"),
            P(None, "tp"),
            P("tp"),
            P("tp"),
            P("tp"),
            P(None, "tp"),
            P("req", None, "tp"),
            P(None, "tp"),
            P(None, "tp"),
            P("req", None, "tp"),
            P("req", "tp", None, None),
            P("tp"),
            P(None, "tp"),
            P("req", None, None),
            P("req", "tp", None),
            P("tp", None),
            P("tp", None),
            P(),
            P(None, ("req", "tp")),
        ),
        out_specs=(
            P("req", "tp"),
            P(("req", "tp"), None),
            P("req", "tp", None, None),
            P("req", None, "tp"),
            P("req", None, "tp"),
            P("req", None),
        ),
        check_vma=False,
    )
```

profile of v0, /device:TPU:0, one launch (start us, length us, event | category | flops | bytes accessed | tf_op | source)
XLA Modules:
  0.0 261.5 jit_solution(11709163570320856122)
XLA Ops:
  7.2 1.2 fusion.24
  8.4 1.9 convolution_convert_fusion.1
  10.3 6.3 %all_gather.24 = bf16[32,1536]{1,0:T(8,128)(2,1)S(1)} all-gather(bf16[32,384]{1,0:T(8,128)(2,1)S(1)} %convolution_convert_fusion.1), channel_id=1, replica_groups=mesh['req'=8,'tp'=4] {'tp'}, dimensions={1}, use_global_device_ids=true | all-gather | bytes 122880 | tf_op jit(solution)/shard_map/all_gather | solution.py:127
  18.6 6.0 %fusion.79 = (bf16[32,256,256]{2,1,0:T(8,128)(2,1)}, bf16[32,256,256]{2,1,0:T(8,128)(2,1)}) fusion(bf16[32,256,512]{2,1,0:T(8,128)(2,1)} %param.41), kind=kLoop, calls=%fused_computation.140 | loop fusion | bytes 16777216 | tf_op jit(solution)/shard_map/slice | solution.py:166
  24.6 6.5 %copy.137 = bf16[32,256,256]{1,2,0:T(8,128)(2,1)} copy(bf16[32,256,256]{2,1,0:T(8,128)(2,1)} %get-tuple-element.233) | data formatting | bytes 8388608
  31.2 2.9 %fusion.80 = (f32[32,2,4]{2,1,0:T(2,128)S(1)}, f32[32,2,4,256]{3,2,1,0:T(4,128)S(1)}) fusion(bf16[32,2,4,128]{3,2,1,0:T(4,128)(2,1)S(1)} %reshape.220, bf16[32,256,2,128]{1,3,2,0:T(8,128)(2,1)} %bitcast.108, pred[32,256]{1,0:T(8,128)(4,1)S(1)} %fusion.52), kind=kOutput, calls=%fused_computation.141 | convolution fusion | flops 16973568 | bytes 4531200 | tf_op jit(solution)/shard_map/rkgd,rskd->rkgs/dot_general | solution.py:61
  35.8 1.4 copy.96
  37.2 1.7 fusion.38
  38.9 1.0 copy.84
  39.9 1.3 reshape.257
  41.3 1.6 fusion.81
  44.3 1.3 max.53
  45.6 1.3 add_convert_fusion
  51.2 1.4 copy.105
  52.6 6.5 %copy.138 = bf16[32,256,256]{1,2,0:T(8,128)(2,1)} copy(bf16[32,256,256]{2,1,0:T(8,128)(2,1)} %get-tuple-element.232) | data formatting | bytes 8388608
  59.1 1.4 fusion.15
  61.4 2.2 fusion.16
  63.6 6.4 %all-gather.2 = bf16[128,2,4,128]{3,2,1,0:T(4,128)(2,1)S(1)} all-gather(bf16[32,2,4,128]{3,2,1,0:T(4,128)(2,1)S(1)} %fusion.16), channel_id=4, replica_groups=mesh['req'=8,'tp'=4] {'tp'}, dimensions={0}, use_global_device_ids=true | all-gather | bytes 327680 | tf_op jit(solution)/shard_map/all_gather | solution.py:22
  71.4 5.4 %all-gather.1 = bf16[128,2,4]{2,1,0:T(2,128)(2,1)S(1)} all-gather(bf16[32,2,4]{2,1,0:T(2,128)(2,1)} %copy.97), channel_id=3, replica_groups=mesh['req'=8,'tp'=4] {'tp'}, dimensions={0}, use_global_device_ids=true | all-gather | bytes 2560 | tf_op jit(solution)/shard_map/all_gather | solution.py:22
  79.0 1.4 copy.90
  80.4 5.4 %all-gather = bf16[128,2,4]{2,1,0:T(2,128)(2,1)S(1)} all-gather(bf16[32,2,4]{2,1,0:T(2,128)(2,1)} %copy.90), channel_id=2, replica_groups=mesh['req'=8,'tp'=4] {'tp'}, dimensions={0}, use_global_device_ids=true | all-gather | bytes 2560 | tf_op jit(solution)/shard_map/all_gather | solution.py:22
  86.5 1.4 copy.108
  88.6 8.4 %while.19 = (s32[]{:T(128)}, f32[32,2,4]{0,2,1:T(4,128)}, f32[32,2,4]{0,2,1:T(4,128)S(1)}, f32[32,2,4,128]{3,2,1,0:T(4,128)S(1)}, bf16[4,32,2,4]{1,3,2,0:T(4,128...) while((s32[]{:T(128)}, f32[32,2,4]{0,2,1:T(4,128)}, ...), condition=%wide.region_8.9_spmd, body=%wide.region_7.8_spmd.sunk | while | flops 133125 | bytes 341143 | solution.py:30
  88.6 1.3 fusion.98
  90.1 1.3 fusion.99
  91.4 1.3 fusion.98
  92.9 1.3 fusion.99
  94.2 1.3 fusion.98
  95.7 1.3 fusion.99
  99.3 1.4 fusion.17
  103.0 1.0 convolution_convert_fusion.3
  106.1 1.3 fusion.20
  108.9 5.2 %all_gather.23 = bf16[32,512]{1,0:T(8,128)(2,1)S(1)} all-gather(bf16[32,128]{1,0:T(8,128)(2,1)S(1)} %fusion.61), channel_id=1, replica_groups=mesh['req'=8,'tp'=4] {'tp'}, dimensions={1}, use_global_device_ids=true | all-gather | bytes 40960 | tf_op jit(solution)/shard_map/all_gather | solution.py:128
  116.2 10.6 %fusion.4 = f32[32,1,6,64]{3,1,2,0:T(1,128)S(1)} fusion(bf16[32,6,64,256]{3,2,1,0:T(8,128)(2,1)} %param.37, f32[32,256]{1,0:T(8,128)} %get-tuple-element.239, f32[32,6,64]{2,1,0:T(8,128)S(1)} %broadcast_multiply_fusion, f32[32,6]{1,0:T(8,128)} %copy.81, bf16[32,256,1,1]{1,0,2,3:T(8,128)(2,1)} %get-tuple-element.238), kind=kOutput, calls=%fused_computation.10 | convolution fusion | flops 50331648 | bytes 6439680 | tf_op jit(solution)/shard_map/rhpn,rn->rhp/dot_general | solution.py:138
  127.5 1.0 reshape.219
  128.7 7.4 %psum.14 = f32[32]{0:T(128)S(1)} all-reduce(f32[32]{0:T(128)S(1)} %multiply_reduce_fusion.2), channel_id=1, replica_groups=mesh['req'=8,'tp'=4] {'tp'}, use_global_device_ids=true, to_apply=%region_2.3 | all-reduce | flops 32 | bytes 256 | tf_op jit(solution)/shard_map/psum | solution.py:145
  136.1 1.8 fusion.54
  137.9 2.2 fusion.11
  140.2 31.8 %all-reduce.2.cloned.1.call-done = bf16[32,2048]{1,0:T(8,128)(2,1)} async-done(((bf16[32,2048]{1,0:T(8,128)(2,1)}), bf16[32,2048]{1,0:T(8,128)(2,1)}) %all-reduce.2.cloned.1.call-update) | async-done | bytes 131088 | tf_op jit(solution)/shard_map/psum | solution.py:181
  172.0 1.1 fusion.21
  173.9 41.2 %all-gather.5.cloned.1.call-done = bf16[256,2048]{1,0:T(8,128)(2,1)} async-done(((bf16[32,2048]{1,0:T(8,128)(2,1)}), bf16[256,2048]{1,0:T(8,128)(2,1)}) %all-gather.5.cloned.1.call-update) | async-done | bytes 1048592 | tf_op jit(solution)/shard_map/all_gather | solution.py:186
  215.1 7.0 %fusion.10 = bf16[32,8,2048]{2,1,0:T(8,128)(2,1)} fusion(bf16[256,2048]{1,0:T(8,128)(2,1)} %all-gather.5.cloned.1.call-done, bf16[2048,2048]{1,0:T(8,128)(2,1)} %param.45), kind=kOutput, calls=%fused_computation.17 | convolution fusion | flops 2148007936 | bytes 10485760 | tf_op jit(solution)/shard_map/dot_general | solution.py:185
  222.1 3.5 %all-to-all-start = ((bf16[32,8,2048]{2,1,0:T(8,128)(2,1)}), bf16[32,8,2048]{2,1,0:T(8,128)(2,1)}, u32[]{:S(2)}, u32[]{:S(2)}) async-start(bf16[32,8,2048]{2,1,0:T(8,128)(2,1)} %fusion.10), calls=%async_computation | async-start | bytes 2097152 | tf_op jit(solution)/shard_map/all_to_all | solution.py:190
  225.6 1.4 slice.85
  227.0 1.3 fusion.53
  229.0 8.1 %fusion.3 = bf16[32,6,64,256]{3,2,1,0:T(8,128)(2,1)} fusion(bf16[32,6,64,256]{3,2,1,0:T(8,128)(2,1)} %param.37, f32[32,256]{1,0:T(8,128)S(1)} %copy-done.11, f32[32,6,64]{2,1,0:T(8,128)S(1)} %copy-done.7, f32[32,6]{1,0:T(8,128)} %copy.81), kind=kLoop, calls=%fused_computation.9 | loop fusion | flops 15728640 | bytes 12665600 | tf_op jit(solution)/shard_map/convert_element_type | solution.py:141
  237.7 14.2 %all-to-all-done = bf16[32,8,2048]{2,1,0:T(8,128)(2,1)} async-done(((bf16[32,8,2048]{2,1,0:T(8,128)(2,1)}), bf16[32,8,2048]{2,1,0:T(8,128)(2,1)}, u32[]{:S(2)}, u32[]{:S(2)}) %all-to-all-start) | async-done | bytes 1048608 | tf_op jit(solution)/shard_map/all_to_all | solution.py:190
  251.8 2.8 %convert_element_type.203 = f32[32,8,2048]{2,1,0:T(8,128)} convert(bf16[32,8,2048]{2,1,0:T(8,128)(2,1)} %all-to-all-done) | non-fusion elementwise | flops 524288 | bytes 3145728 | tf_op jit(solution)/shard_map/convert_element_type | solution.py:192
  (106 shorter events, 29.2 us)
Async XLA Ops:
  7.2 92.1 %copy-start = (bf16[2048,2,384]{2,1,0:T(2,128)(2,1)S(1)}, bf16[2048,2,384]{2,1,0:T(2,128)(2,1)}, u32[]{:S(2)}) copy-start(bf16[2048,2,384]{2,1,0:T(2,128)(2,1)} %param.27) | copy-start | bytes 9437188
  7.2 164.8 %all-reduce.2.cloned.1.call-start = ((), (), s32[]{:S(2)}) async-start(), calls=%async_computation.1 | async-start | bytes 262144 | tf_op jit(solution)/shard_map/psum | solution.py:181
  8.4 8.2 %copy-start.20 = (f32[32]{0:T(128)}, f32[32]{0:T(128)S(1)}, u32[]{:S(2)}) copy-start(f32[32]{0:T(128)S(1)} %add_rsqrt_fusion.2) | copy-start | bytes 388
  16.6 0.7 copy-start.5
  31.2 6.0 %copy-start.14 = (pred[32,256]{1,0:T(8,128)(4,1)}, pred[32,256]{1,0:T(8,128)(4,1)S(1)}, u32[]{:S(2)}) copy-start(pred[32,256]{1,0:T(8,128)(4,1)S(1)} %fusion.52) | copy-start | bytes 24580
  34.2 24.9 %copy-start.4 = (f32[32,2,4,256]{3,2,1,0:T(4,128)}, f32[32,2,4,256]{3,2,1,0:T(4,128)S(1)}, u32[]{:S(2)}) copy-start(f32[32,2,4,256]{3,2,1,0:T(4,128)S(1)} %get-tuple-element.246) | copy-start | bytes 786436
  51.2 7.9 %copy-start.16 = (f32[32,2,4]{2,1,0:T(2,128)S(1)}, f32[32,2,4]{2,1,0:T(2,128)}, u32[]{:S(2)}) copy-start(f32[32,2,4]{2,1,0:T(2,128)} %copy.100) | copy-start | bytes 3076
  52.6 7.9 %copy-start.15 = (pred[32,256]{1,0:T(8,128)(4,1)S(1)}, pred[32,256]{1,0:T(8,128)(4,1)}, u32[]{:S(2)}) copy-start(pred[32,256]{1,0:T(8,128)(4,1)} %copy-done.14) | copy-start | bytes 24580
  59.1 2.3 copy-start.1
  59.1 2.3 copy-start.17
  59.1 11.5 %copy-start.19 = (bf16[32,2,4]{0,2,1:T(4,128)(2,1)S(1)}, bf16[32,2,4]{0,2,1:T(4,128)(2,1)}, u32[]{:S(2)}) copy-start(bf16[32,2,4]{0,2,1:T(4,128)(2,1)} %get-tuple-element.228) | copy-start | bytes 1540
  60.5 38.8 %copy-start.2 = (bf16[32,2048]{1,0:T(8,128)(2,1)S(1)}, bf16[32,2048]{1,0:T(8,128)(2,1)}, u32[]{:S(2)}) copy-start(bf16[32,2048]{1,0:T(8,128)(2,1)} %param.24) | copy-start | bytes 393220
  63.6 37.8 %copy-start.8 = (bf16[32,3,384]{2,0,1:T(8,128)(2,1)S(1)}, bf16[32,3,384]{2,0,1:T(8,128)(2,1)}, u32[]{:S(2)}) copy-start(bf16[32,3,384]{2,0,1:T(8,128)(2,1)} %param.33) | copy-start | bytes 221188
  69.9 0.7 copy-start.3
  100.7 26.1 %copy-start.9 = (bf16[32,1,384]{2,0,1:T(8,128)(2,1)}, bf16[32,1,384]{2,0,1:T(8,128)(2,1)S(1)}, u32[]{:S(2)}) copy-start(bf16[32,1,384]{2,0,1:T(8,128)(2,1)S(1)} %get-tuple-element.237) | copy-start | bytes 73732
  107.4 19.4 %copy-start.12 = (bf16[32,1,128]{2,0,1:T(8,128)(2,1)}, bf16[32,1,128]{2,0,1:T(8,128)(2,1)S(1)}, u32[]{:S(2)}) copy-start(bf16[32,1,128]{2,0,1:T(8,128)(2,1)S(1)} %fusion.20) | copy-start | bytes 24580
  116.2 10.6 %copy-start.6 = (f32[32,6,64]{2,1,0:T(8,128)}, f32[32,6,64]{2,1,0:T(8,128)S(1)}, u32[]{:S(2)}) copy-start(f32[32,6,64]{2,1,0:T(8,128)S(1)} %broadcast_multiply_fusion) | copy-start | bytes 147460
  116.2 10.6 %copy-start.22 = (f32[6]{0:T(128)S(1)}, f32[6]{0:T(128)}, u32[]{:S(2)}) copy-start(f32[6]{0:T(128)} %param.31) | copy-start | bytes 76
  116.2 19.9 %copy-start.21 = (f32[384]{0:T(512)S(1)}, f32[384]{0:T(512)}, u32[]{:S(2)}) copy-start(f32[384]{0:T(512)} %param.38) | copy-start | bytes 4612
  116.2 56.9 %copy-start.18 = (f32[2048]{0:T(1024)S(1)}, f32[2048]{0:T(1024)}, u32[]{:S(2)}) copy-start(f32[2048]{0:T(1024)} %param.44) | copy-start | bytes 24580
  140.1 75.0 %all-gather.5.cloned.1.call-start = ((), (), s32[]{:S(2)}) async-start(), calls=%async_computation.2 | async-start | bytes 1179648 | tf_op jit(solution)/shard_map/all_gather | solution.py:186
  173.9 53.1 %copy-start.13 = (bf16[32,1,128]{2,0,1:T(8,128)(2,1)S(1)}, bf16[32,1,128]{2,0,1:T(8,128)(2,1)}, u32[]{:S(2)}) copy-start(bf16[32,1,128]{2,0,1:T(8,128)(2,1)} %copy-done.12) | copy-start | bytes 24580
  173.9 54.5 %copy-start.10 = (bf16[32,1,384]{2,0,1:T(8,128)(2,1)S(1)}, bf16[32,1,384]{2,0,1:T(8,128)(2,1)}, u32[]{:S(2)}) copy-start(bf16[32,1,384]{2,0,1:T(8,128)(2,1)} %copy-done.9) | copy-start | bytes 73732
  173.9 55.1 %copy-start.7 = (f32[32,6,64]{2,1,0:T(8,128)S(1)}, f32[32,6,64]{2,1,0:T(8,128)}, u32[]{:S(2)}) copy-start(f32[32,6,64]{2,1,0:T(8,128)} %copy-done.6) | copy-start | bytes 147460
  173.9 55.1 %copy-start.11 = (f32[32,256]{1,0:T(8,128)S(1)}, f32[32,256]{1,0:T(8,128)}, u32[]{:S(2)}) copy-start(f32[32,256]{1,0:T(8,128)} %get-tuple-element.239) | copy-start | bytes 98308
  222.1 29.7 %all-to-all-start = ((bf16[32,8,2048]{2,1,0:T(8,128)(2,1)}), bf16[32,8,2048]{2,1,0:T(8,128)(2,1)}, u32[]{:S(2)}, u32[]{:S(2)}) async-start(bf16[32,8,2048]{2,1,0:T(8,128)(2,1)} %fusion.10), calls=%async_computation | async-start | bytes 2097152 | tf_op jit(solution)/shard_map/all_to_all | solution.py:190
Sparse Core Ops, SparseCore 0:
  140.2 31.7 all-reduce.1
  174.9 40.1 all-gather.4
where the time goes:
time: 264 us; the launch traced here: 261 us
  waiting for transfers between devices  87.2 us (33%)
  local copies, waits for them, and re-layouts  46.1 us (17%)
  other arithmetic  37.1 us (14%)
  matrix products  37 us (14%)
  blocking collectives  36.1 us (14%)
  between operations  14.4 us (5%)
  starting transfers between devices  3.56 us (1%)
    all_gather x1, waiting for transfers between devices, body(): lax.all_gather(final_rows, 'req', axis=0, tiled=True)  41.2 us
    psum x1, waiting for transfers between devices, body(): lax.psum(mixed_rows.astype(jnp.bfloat16), 'tp').astype(jnp.float32)  31.8 us
    all_gather x3, blocking collectives, combined_all(): lax.all_gather(part.astype(kind), axis)  17.2 us
    unnamed x48, local copies, waits for them, and re-layouts  15.3 us
    all_to_all x1, waiting for transfers between devices, body(): lax.all_to_all(vocab_logits.astype(jnp.bfloat16), ('req', 'tp'), split_ax...  14.2 us
    dot_general x1, matrix products, body(): jnp.einsum('rhpn,rn->rhp', updated, output_vec, precision=lax.Precision.H...  10.6 us
    convert_element_type x1, other arithmetic, body(): new_scan_state = updated.astype(jnp.bfloat16)  8.08 us
    psum x1, blocking collectives, body(): square_total = lax.psum(jnp.sum(gated_rows * gated_rows, axis=1), 'tp')  7.38 us
  transfers between devices with their start and end apart: 3, of which 3 were waited for; matrix products, arithmetic and copies ran while one was open for 5% of the time, Pallas kernels for 0%

commit v1 on v0

v1 whole, which is shorter than its diff:
```python
import functools

import jax
import jax.numpy as jnp
from jax import lax
from jax.experimental import pallas as pl
from jax.experimental.pallas import tpu as pltpu
from jax.sharding import PartitionSpec as P

MH = 24
MP = 64
NS = 256
QH = 8
KVH = 2
HD = 128
WIN = 1024
SINK = 4
BR = 8
EXTRA = 16

EPSILON = 1e-05
NEG_BIG = -1e30
MESH = pl.DeviceIdType.MESH
NT = (((1,), (1,)), ((), ()))


def norm_rows(values, gain):
    widened = values.astype(jnp.float32)
    mean_sq = jnp.mean(widened * widened, axis=-1, keepdims=True)
    return (widened * lax.rsqrt(mean_sq + EPSILON) * gain).astype(jnp.bfloat16)


def conv_apply(old_state, fresh_row, taps):
    window = jnp.concatenate([old_state, fresh_row[:, None, :]], axis=1)
    mixed_rows = jnp.einsum("rkc,kc->rc", window, taps, preferred_element_type=jnp.float32)
    return (jax.nn.silu(mixed_rows), window[:, 1:, :])


def mixer_kernel(
    qkv_ref, extra_ref, mask_ref, window_ref, state_ref, coup_ref, x_ref, step_ref, decay_ref,
    gate_ref, skip_ref, new_state_ref, summed_ref, stats_ref, gated_ref, heads_scr,
):
    half = KVH * HD
    group = QH // KVH
    for h in range(QH):
        heads_scr[pl.ds(h, BR, stride=QH), :] = qkv_ref[:, h * HD : (h + 1) * HD].astype(jnp.float32)
    head_row = lax.broadcasted_iota(jnp.int32, (QH, HD), 0)
    lane = lax.broadcasted_iota(jnp.int32, (QH, HD), 1)
    first_half = head_row < group
    x = x_ref[...]
    step_x = step_ref[...] * x
    decay = decay_ref[...]
    step_x_t = step_x.T
    decay_t = decay.T
    coup = coup_ref[...]
    out_rows = coup[:, NS:]
    in_f32 = coup[:, :NS].astype(jnp.float32)
    both = jnp.sum(in_f32 * out_rows.astype(jnp.float32), axis=1, keepdims=True)
    read_rows = []
    for j in range(BR):
        q = heads_scr[j * QH : (j + 1) * QH, :]
        wide = jnp.concatenate(
            [jnp.where(first_half, q, 0.0), jnp.where(first_half, 0.0, q)], axis=1
        ).astype(jnp.bfloat16)
        s1 = lax.dot_general(
            wide, window_ref[j, :, :half], NT, preferred_element_type=jnp.float32
        ) * HD ** (-0.5)
        s2 = lax.dot_general(
            wide, extra_ref[j, :, :half], NT, preferred_element_type=jnp.float32
        ) * HD ** (-0.5)
        slots = window_ref.shape[1]
        live1 = jnp.broadcast_to(mask_ref[j : j + 1, :slots], s1.shape) > 0.5
        live2 = jnp.broadcast_to(mask_ref[j : j + 1, slots : slots + EXTRA], s2.shape) > 0.5
        s1 = jnp.where(live1, s1, NEG_BIG)
        s2 = jnp.where(live2, s2, NEG_BIG)
        peak = jnp.maximum(
            jnp.max(s1, axis=1, keepdims=True), jnp.max(s2, axis=1, keepdims=True)
        )
        w1 = jnp.where(live1, jnp.exp(s1 - peak), 0.0)
        w2 = jnp.where(live2, jnp.exp(s2 - peak), 0.0)
        total = jnp.sum(w1, axis=1, keepdims=True) + jnp.sum(w2, axis=1, keepdims=True)
        acc = jnp.dot(
            w1.astype(jnp.bfloat16), window_ref[j, :, half:], preferred_element_type=jnp.float32
        ) + jnp.dot(
            w2.astype(jnp.bfloat16), extra_ref[j, :, half:], preferred_element_type=jnp.float32
        )
        heads_scr[j * QH : (j + 1) * QH, :] = jnp.where(first_half, acc[:, :HD], acc[:, HD:])
        stats_ref[j : j + 1, :] = jnp.sum(
            jnp.where(lane == head_row, peak, 0.0)
            + jnp.where(lane == head_row + QH, total, 0.0),
            axis=0,
            keepdims=True,
        )
        state = state_ref[j]
        read_rows.append(
            lax.dot_general(out_rows, state, NT, preferred_element_type=jnp.float32)[j : j + 1, :]
        )
        new_state_ref[j] = (
            decay_t[:, j : j + 1] * state.astype(jnp.float32)
            + step_x_t[:, j : j + 1] * in_f32[j : j + 1, :]
        ).astype(jnp.bfloat16)
    per_chunk = summed_ref.shape[2] // HD
    for h in range(QH):
        summed_ref[h // per_chunk, :, (h % per_chunk) * HD : (h % per_chunk + 1) * HD] = heads_scr[
            pl.ds(h, BR, stride=QH), :
        ].astype(jnp.bfloat16)
    readout = decay * jnp.concatenate(read_rows, axis=0) + step_x * both + skip_ref[...] * x
    gate = gate_ref[...].astype(jnp.float32)
    gated = readout * (gate / (1.0 + jnp.exp(-gate)))
    gated_ref[...] = gated
    square = jnp.sum(gated * gated, axis=1, keepdims=True)
    stats_ref[...] = jnp.where(
        lax.broadcasted_iota(jnp.int32, stats_ref.shape, 1) == 2 * QH, square, stats_ref[...]
    )


def mixer(qkv, extra, mask, window, state, coup, x, step, decay, gate, skip, tp_size):
    rows, units = x.shape
    slots = window.shape[1]
    row = lambda width: pl.BlockSpec((BR, width), lambda i: (i, 0))
    cube = lambda a: pl.BlockSpec((BR,) + a.shape[1:], lambda i: (i, 0, 0))
    chunk = QH * HD // tp_size
    return pl.pallas_call(
        mixer_kernel,
        grid=(rows // BR,),
        in_specs=[
            row(qkv.shape[1]), cube(extra), row(mask.shape[1]), cube(window), cube(state),
            row(coup.shape[1]), row(units), row(units), row(units), row(units),
            pl.BlockSpec((1, units), lambda i: (0, 0)),
        ],
        out_specs=[
            cube(state), pl.BlockSpec((tp_size, BR, chunk), lambda i: (0, i, 0)), row(128), row(units),
        ],
        out_shape=[
            jax.ShapeDtypeStruct(state.shape, jnp.bfloat16),
            jax.ShapeDtypeStruct((tp_size, rows, chunk), jnp.bfloat16),
            jax.ShapeDtypeStruct((rows, 128), jnp.float32),
            jax.ShapeDtypeStruct((rows, units), jnp.float32),
        ],
        scratch_shapes=[pltpu.VMEM((BR * QH, HD), jnp.float32)],
        compiler_params=pltpu.CompilerParams(vmem_limit_bytes=40 << 20),
    )(qkv, extra, mask, window, state, coup, x, step, decay, gate, skip)


def joint_kernel(
    tp_size, req_size, summed_ref, stats_ref, gated_ref, mixer_gain_ref, mamba_out_ref,
    attention_out_ref, residual_ref, final_gain_ref, new_residual_ref, final_ref,
    sum_buf, stat_buf, part_out, part_buf, gather, sum_s, sum_r, stat_s, stat_r, part_s, part_r,
    gat_s, gat_r,
):
    r = lax.axis_index("req")
    t = lax.axis_index("tp")
    rows = gated_ref.shape[0]
    width = new_residual_ref.shape[1]
    peers = [lax.rem(t + k, tp_size) for k in range(tp_size)]
    reqs = [lax.rem(r + k, req_size) for k in range(req_size)]
    barrier = pltpu.get_barrier_semaphore()
    for k in range(1, tp_size):
        pl.semaphore_signal(barrier, inc=1, device_id=(r, peers[k]), device_id_type=MESH)
    for k in range(1, req_size):
        pl.semaphore_signal(barrier, inc=1, device_id=(reqs[k], t), device_id_type=MESH)
    pl.semaphore_wait(barrier, tp_size - 1 + req_size - 1)

    def send(src, dst, ssem, rsem, where):
        copy = pltpu.make_async_remote_copy(
            src_ref=src, dst_ref=dst, send_sem=ssem, recv_sem=rsem,
            device_id=where, device_id_type=MESH,
        )
        copy.start()
        return copy

    first = []
    for k in range(1, tp_size):
        where = (r, peers[k])
        first.append(send(stats_ref, stat_buf.at[k], stat_s.at[k], stat_r.at[k], where))
        first.append(send(summed_ref.at[peers[k]], sum_buf.at[k], sum_s.at[k], sum_r.at[k], where))
    for copy in first:
        copy.wait()
    stats = [stats_ref[...]] + [stat_buf[k] for k in range(1, tp_size)]
    sums = [summed_ref[t].astype(jnp.float32)] + [
        sum_buf[k].astype(jnp.float32) for k in range(1, tp_size)
    ]
    lane = lax.broadcasted_iota(jnp.int32, (rows, 128), 1)
    local_heads = QH // tp_size
    pieces = []
    for hl in range(local_heads):
        h = t * local_heads + hl
        peaks = [jnp.sum(jnp.where(lane == h, s, 0.0), axis=1, keepdims=True) for s in stats]
        totals = [jnp.sum(jnp.where(lane == h + QH, s, 0.0), axis=1, keepdims=True) for s in stats]
        top = functools.reduce(jnp.maximum, peaks)
        scales = [jnp.exp(p - top) for p in peaks]
        below = functools.reduce(jnp.add, [a * b for a, b in zip(scales, totals)])
        above = functools.reduce(
            jnp.add, [a * b[:, hl * HD : (hl + 1) * HD] for a, b in zip(scales, sums)]
        )
        pieces.append((above / below).astype(jnp.bfloat16))
    attended = jnp.concatenate(pieces, axis=1)
    square = functools.reduce(jnp.add, [s[:, 2 * QH : 2 * QH + 1] for s in stats])
    mamba = (
        gated_ref[...] * lax.rsqrt(square / (MH * MP) + EPSILON) * mixer_gain_ref[...]
    ).astype(jnp.bfloat16)

    def partial(p):
        cols = pl.ds(pl.multiple_of(p * width, 128), width)
        return jnp.dot(mamba, mamba_out_ref[:, cols], preferred_element_type=jnp.float32) + jnp.dot(
            attended, attention_out_ref[:, cols], preferred_element_type=jnp.float32
        )

    second = []
    for k in range(1, tp_size):
        part_out[k] = partial(peers[k]).astype(jnp.bfloat16)
        second.append(
            send(part_out.at[k], part_buf.at[k], part_s.at[k], part_r.at[k], (r, peers[k]))
        )
    mixed = partial(t)
    for k in range(1, tp_size):
        second[k - 1].wait()
        mixed = mixed + part_buf[k].astype(jnp.float32)
    own = pl.ds(pl.multiple_of(t * width, 128), width)
    fresh = (residual_ref[:, own].astype(jnp.float32) + mixed).astype(jnp.bfloat16)
    new_residual_ref[...] = fresh
    gather[0, 0] = fresh

    beside = t + 1 - 2 * lax.rem(t, 2)
    across = lax.rem(t + 2, tp_size)
    owner = [t, beside, across, lax.rem(beside + 2, tp_size)]
    along = [None]
    for k in range(1, req_size):
        along.append(
            send(gather.at[0, 0], gather.at[k, 0], gat_s.at[k, 0], gat_r.at[k, 0], (reqs[k], t))
        )
    over, near, far = [], [], []
    for k in range(req_size):
        if k:
            along[k].wait_recv()
        over.append(
            send(gather.at[k, 0], gather.at[k, 2], gat_s.at[k, 2], gat_r.at[k, 2], (r, across))
        )
        near.append(
            send(gather.at[k, 0], gather.at[k, 1], gat_s.at[k, 1], gat_r.at[k, 1], (r, beside))
        )
    for k in range(req_size):
        over[k].wait_recv()
        far.append(
            send(gather.at[k, 2], gather.at[k, 3], gat_s.at[k, 3], gat_r.at[k, 3], (r, beside))
        )
    for k in range(req_size):
        near[k].wait_recv()
        far[k].wait_recv()
        values = [gather[k, i].astype(jnp.float32) for i in range(4)]
        mean = functools.reduce(
            jnp.add, [jnp.sum(v * v, axis=1, keepdims=True) for v in values]
        ) / (width * tp_size)
        scale = lax.rsqrt(mean + EPSILON)
        source = lax.rem(r + req_size - k, req_size)
        at = pl.ds(pl.multiple_of(source * rows, rows), rows)
        for i in range(4):
            cols = pl.ds(pl.multiple_of(owner[i] * width, 128), width)
            final_ref[at, cols] = (values[i] * scale * final_gain_ref[:, cols]).astype(jnp.bfloat16)
    for k in range(req_size):
        if k:
            along[k].wait_send()
        over[k].wait_send()
        near[k].wait_send()
        far[k].wait_send()


def joint(summed, stats, gated, mixer_gain, mamba_out, attention_out, residual, final_gain):
    tp_size = lax.axis_size("tp")
    req_size = lax.axis_size("req")
    rows, model = residual.shape
    width = model // tp_size
    chunk = summed.shape[2]
    dma = lambda *shape: pltpu.SemaphoreType.DMA(shape)
    vmem = pl.BlockSpec(memory_space=pltpu.VMEM)
    return pl.pallas_call(
        functools.partial(joint_kernel, tp_size, req_size),
        in_specs=[vmem] * 8,
        out_specs=[vmem] * 2,
        out_shape=[
            jax.ShapeDtypeStruct((rows, width), jnp.bfloat16),
            jax.ShapeDtypeStruct((rows * req_size, model), jnp.bfloat16),
        ],
        scratch_shapes=[
            pltpu.VMEM((tp_size, rows, chunk), jnp.bfloat16),
            pltpu.VMEM((tp_size, rows, 128), jnp.float32),
            pltpu.VMEM((tp_size, rows, width), jnp.bfloat16),
            pltpu.VMEM((tp_size, rows, width), jnp.bfloat16),
            pltpu.VMEM((req_size, 4, rows, width), jnp.bfloat16),
            dma(tp_size), dma(tp_size), dma(tp_size), dma(tp_size), dma(tp_size), dma(tp_size),
            dma(req_size, 4), dma(req_size, 4),
        ],
        compiler_params=pltpu.CompilerParams(
            collective_id=1, has_side_effects=True, vmem_limit_bytes=40 << 20
        ),
    )(summed, stats, gated, mixer_gain[None], mamba_out, attention_out, residual, final_gain[None])


def body(
    residual,
    cache_lengths,
    input_gain,
    inner_weight,
    step_weight,
    step_bias,
    decay_log,
    skip_gain,
    conv_weight,
    conv_state,
    coupling_weight,
    coupling_conv,
    coupling_state,
    scan_state,
    mixer_gain,
    attention_weight,
    sink_cache,
    window_cache,
    mamba_out,
    attention_out,
    final_gain,
    output_head,
):
    row_count = residual.shape[0]
    tp_size = lax.axis_size("tp")
    tp_index = lax.axis_index("tp")
    local_units = inner_weight.shape[2]
    half_width = KVH * HD
    normed = norm_rows(residual, input_gain)
    projected = jnp.einsum(
        "rd,dtc->rtc", normed, inner_weight, preferred_element_type=jnp.float32
    ).astype(jnp.bfloat16)
    gate_rows = lax.optimization_barrier(projected[:, 0, :])
    x_rows, new_conv_state = conv_apply(conv_state, projected[:, 1, :], conv_weight)
    step_rows = lax.optimization_barrier(
        jnp.dot(normed, step_weight, preferred_element_type=jnp.float32).astype(jnp.bfloat16)
    )
    step_size = jax.nn.softplus(step_rows.astype(jnp.float32) + step_bias)
    decay_rate = jnp.exp(-step_size * jnp.exp(decay_log))
    coupling_pre = jnp.dot(normed, coupling_weight, preferred_element_type=jnp.float32).astype(
        jnp.bfloat16
    )
    coupling_rows, new_coupling_state = conv_apply(coupling_state, coupling_pre, coupling_conv)
    qkv_local = jnp.dot(normed, attention_weight, preferred_element_type=jnp.float32).astype(
        jnp.bfloat16
    )
    qkv_rows, coupling_all = (
        lax.all_gather(qkv_local, "tp", axis=1, tiled=True),
        lax.all_gather(coupling_rows.astype(jnp.bfloat16), "tp", axis=1, tiled=True),
    )
    new_key_value = qkv_rows[:, QH * HD :]
    window_slots = window_cache.shape[1]
    slot_index = tp_index * window_slots + jnp.arange(window_slots, dtype=jnp.int32)
    length_column = cache_lengths[:, None]
    back_steps = (length_column - 1 - slot_index[None, :]) % WIN
    position = length_column - 1 - back_steps
    live_mask = (position >= SINK) & (back_steps != WIN - 1)
    extra_live = (jnp.arange(128) < SINK + 1) & (tp_index == 0)
    mask = jnp.concatenate(
        [live_mask, jnp.broadcast_to(extra_live, (row_count, 128))], axis=1
    ).astype(jnp.float32)
    extra = jnp.concatenate(
        [
            sink_cache,
            new_key_value[:, None, :],
            jnp.zeros((row_count, EXTRA - SINK - 1, 2 * half_width), jnp.bfloat16),
        ],
        axis=1,
    )
    spread = lambda per_head: jnp.repeat(per_head, MP, axis=-1)
    new_state, summed, stats, gated = mixer(
        qkv_rows, extra, mask, window_cache, scan_state.reshape(row_count, local_units, NS),
        coupling_all, x_rows, spread(step_size), spread(decay_rate), gate_rows,
        spread(skip_gain)[None], tp_size,
    )
    new_scan_state = new_state.reshape(scan_state.shape)
    new_residual, final_rows = joint(
        summed, stats, gated, mixer_gain, mamba_out, attention_out, residual, final_gain
    )
    vocab_logits = jnp.dot(
        final_rows,
        output_head,
        preferred_element_type=jnp.float32,
    )
    logits = lax.all_to_all(
        vocab_logits.astype(jnp.bfloat16), ("req", "tp"), split_axis=0, concat_axis=1, tiled=True
    ).astype(vocab_logits.dtype)
    return (new_residual, logits, new_scan_state, new_conv_state, new_coupling_state, new_key_value)


def solution(mesh):
    return jax.shard_map(
        body,
        mesh=mesh,
        in_specs=(
            P("req", None),
            P("req"),
            P(),
            P(None, None, "tp"),
            P(None, "tp"),
            P("tp"),
            P("tp"),
            P("tp"),
            P(None, "tp"),
            P("req", None, "tp"),
            P(None, "tp"),
            P(None, "tp"),
            P("req", None, "tp"),
            P("req", "tp", None, None),
            P("tp"),
            P(None, "tp"),
            P("req", None, None),
            P("req", "tp", None),
            P("tp", None),
            P("tp", None),
            P(),
            P(None, ("req", "tp")),
        ),
        out_specs=(
            P("req", "tp"),
            P(("req", "tp"), None),
            P("req", "tp", None, None),
            P("req", None, "tp"),
            P("req", None, "tp"),
            P("req", None),
        ),
        check_vma=False,
    )
```

time: 264 us -> 115 us (0.44)
  waiting for transfers between devices: 87.2 us -> 24.3 us
  Pallas kernels: 0 us -> 38.6 us
  local copies, waits for them, and re-layouts: 46.1 us -> 11.6 us
  other arithmetic: 37.1 us -> 10.8 us
  blocking collectives: 36.1 us -> 11.7 us
  matrix products: 37 us -> 12.8 us
  between operations: 14.4 us -> 0.84 us
    all_gather x1 -> x0, waiting for transfers between devices: 41.2 us -> none  [body(): lax.all_gather(final_rows, 'req', axis=0, tiled=True)]
    pallas_call x0 -> x2, Pallas kernels: none -> 38.6 us  [the longest x1 24.2 us: joint(): pl.pallas_call(functools.partial(joint_kernel, tp_size, req_size), in_spe...]
    psum x1 -> x0, waiting for transfers between devices: 31.8 us -> none  [body(): lax.psum(mixed_rows.astype(jnp.bfloat16), 'tp').astype(jnp.float32)]
    dot_general x9 -> x1, matrix products: 31.4 us -> 6.74 us  [body(): jnp.dot(final_rows, output_head, preferred_element_type=jnp.float32)]
    all_gather x3 -> x0, blocking collectives: 17.2 us -> none  [combined_all(): lax.all_gather(part.astype(kind), axis)]
    convert_element_type x8 -> x1, other arithmetic: 12.9 us -> 0.01 us  [body(): mask = jnp.concatenate([live_mask, jnp.broadcast_to(extra_live, (row_coun...]
    unnamed x48 -> x23, local copies, waits for them, and re-layouts: 15.3 us -> 4 us
    all_to_all x1, waiting for transfers between devices: 14.2 us -> 24.3 us  [body(): lax.all_to_all(vocab_logits.astype(jnp.bfloat16), ('req', 'tp'), split_ax...]
  transfers between devices with their start and end apart: 3 -> 1, of which waited for: 3 -> 1; matrix products, arithmetic and copies ran while one was open for 5% -> 2% of each run, Pallas kernels for 0% -> 0%
where the time goes in v1:
time: 115 us
  Pallas kernels  38.6 us (34%)
  waiting for transfers between devices  24.3 us (21%)
  matrix products  12.8 us (11%)
  blocking collectives  11.7 us (10%)
  local copies, waits for them, and re-layouts  11.6 us (10%)
  other arithmetic  10.8 us (9%)
  starting transfers between devices  4.04 us (4%)
    all_to_all x1, waiting for transfers between devices, body(): lax.all_to_all(vocab_logits.astype(jnp.bfloat16), ('req', 'tp'), split_ax...  24.3 us
    pallas_call x1, Pallas kernels, joint(): pl.pallas_call(functools.partial(joint_kernel, tp_size, req_size), in_spe...  24.2 us
    pallas_call x1, Pallas kernels, mixer(): pl.pallas_call(mixer_kernel, grid=(rows // BR,), in_specs=[row(qkv.shape[...  14.4 us
    dot_general x1, matrix products, body(): jnp.dot(final_rows, output_head, preferred_element_type=jnp.float32)  6.74 us
    all_gather x1, blocking collectives, body(): lax.all_gather(coupling_rows.astype(jnp.bfloat16), 'tp', axis=1, tiled=True)  6.08 us
    all_gather x1, blocking collectives, body(): lax.all_gather(qkv_local, 'tp', axis=1, tiled=True)  5.64 us
    all_to_all x1, starting transfers between devices, body(): lax.all_to_all(vocab_logits.astype(jnp.bfloat16), ('req', 'tp'), split_ax...  4.04 us
    unnamed x23, local copies, waits for them, and re-layouts  4 us
  transfers between devices with their start and end apart: 1, of which 1 were waited for; matrix products, arithmetic and copies ran while one was open for 2% of the time, Pallas kernels for 0%

profile of v1, /device:TPU:0, one launch (start us, length us, event | category | flops | bytes accessed | tf_op | source)
XLA Modules:
  0.0 114.7 jit_solution(9903817462879648021)
XLA Ops:
  0.6 0.0 copy-start
  0.7 0.5 compare_and_fusion
  1.2 0.9 broadcast_add_fusion
  2.1 0.7 exp.21
  2.7 1.0 fusion.7
  3.8 0.7 broadcast_in_dim.40.mixer_gain_ref
  4.5 1.1 convolution_convert_fusion.3
  5.6 0.7 bitcast_convert_fusion.1
  6.4 0.7 broadcast_in_dim.39
  7.1 0.1 broadcast_in_dim_reshape.3.skip_ref
  7.2 0.7 bitcast_convert_fusion
  7.8 1.4 %fusion.6 = bf16[32,1,128]{2,0,1:T(8,128)(2,1)S(1)} fusion(bf16[2048,128]{1,0:T(8,128)(2,1)} %param.32, bf16[32,2048]{1,0:T(8,128)(2,1)} %residual_ref.1, f32[2048]{0:T(1024)} %param.24, f32[32]{0:T(128)S(1)} %add_rsqrt_fusion), kind=kOutput, calls=%fused_computation.7 | convolution fusion | flops 17043456 | bytes 671872 | tf_op jit(solution)/shard_map/dot_general | solution.py:339
  9.2 0.7 multiply_exponential_fusion
  10.0 0.7 copy.34
  10.7 0.7 multiply_reduce_fusion.1
  11.5 0.1 copy.33
  11.6 6.1 %all_gather.7.coup_ref = bf16[32,512]{1,0:T(8,128)(2,1)S(1)} all-gather(bf16[32,128]{1,0:T(8,128)(2,1)S(1)} %fusion.23), channel_id=1, replica_groups=mesh['req'=8,'tp'=4] {'tp'}, dimensions={1}, use_global_device_ids=true | all-gather | bytes 40960 | tf_op jit(solution)/shard_map/all_gather | solution.py:348
  17.6 1.9 %convolution_convert_fusion.1 = bf16[32,384]{1,0:T(8,128)(2,1)S(1)} fusion(bf16[2048,384]{1,0:T(8,128)(2,1)} %param.37, bf16[32,2048]{1,0:T(8,128)(2,1)} %residual_ref.1, f32[2048]{0:T(1024)} %param.24, f32[32]{0:T(128)S(1)} %add_rsqrt_fusion), kind=kOutput, calls=%fused_computation.5 | convolution fusion | flops 50606080 | bytes 1736832 | tf_op jit(solution)/shard_map/dot_general | solution.py:343
  19.5 1.6 %fusion.3 = bf16[32,2,384]{2,0,1:T(8,128)(2,1)S(1)} fusion(bf16[2048,2,384]{2,1,0:T(2,128)(2,1)S(1)} %copy-done, bf16[32,2048]{1,0:T(8,128)(2,1)} %residual_ref.1, f32[2048]{0:T(1024)} %param.24, f32[32]{0:T(128)S(1)} %add_rsqrt_fusion), kind=kOutput, calls=%fused_computation.4 | convolution fusion | flops 100950016 | bytes 3334272 | tf_op jit(solution)/shard_map/rd,dtc->rtc/dot_general | solution.py:329
  21.2 0.0 copy-start.8
  21.2 0.6 copy-done.8
  21.8 5.6 %all_gather.6.qkv_ref = bf16[32,1536]{1,0:T(8,128)(2,1)S(1)} all-gather(bf16[32,384]{1,0:T(8,128)(2,1)S(1)} %convolution_convert_fusion.1), channel_id=1, replica_groups=mesh['req'=8,'tp'=4] {'tp'}, dimensions={1}, use_global_device_ids=true | all-gather | bytes 122880 | tf_op jit(solution)/shard_map/all_gather | solution.py:347
  27.5 0.7 copy.31
  28.1 0.1 broadcast_in_dim.37
  28.2 0.1 reshape.47.step_ref
  28.3 1.5 %broadcast_in_dim.38 = f32[32,6,64]{2,1,0:T(8,128)} broadcast(f32[32,6]{1,0:T(8,128)} %copy.34), dimensions={0,1} | broadcast | bytes 49920 | tf_op jit(solution)/shard_map/broadcast_in_dim | solution.py:369
  29.8 1.0 reshape.48.decay_ref
  30.8 0.7 pad.5.clone
  31.4 0.1 pad.8.clone
  31.5 0.1 fusion.18
  31.6 1.2 %maximum_maximum_fusion.extra_ref = bf16[32,16,512]{2,1,0:T(8,128)(2,1)S(1)} fusion(bf16[32,1,512]{2,1,0:T(2,128)(2,1)} %copy.31, bf16[32,4,512]{2,1,0:T(4,128)(2,1)} %param.38, bf16[16]{0:T(256)(128)(2,1)S(1)} %pad.8.clone), kind=kLoop, calls=%fused_computation.9 | loop fusion | flops 1572864 | bytes 688160 | tf_op jit(solution)/shard_map/concatenate | solution.py:361
  32.8 0.0 copy-start.1
  32.8 2.8 %copy-done.1 = bf16[32,6,64,256]{3,2,1,0:T(8,128)(2,1)S(1)} copy-done((bf16[32,6,64,256]{3,2,1,0:T(8,128)(2,1)S(1)}, bf16[32,6,64,256]{3,2,1,0:T(8,128)(2,1)}, u32[]{:S(2)}) %copy-start.1) | copy-done | bytes 6291480
  35.6 14.4 %shard_map.253 = (bf16[32,384,256]{2,1,0:T(8,128)(2,1)}, bf16[4,32,256]{2,1,0:T(8,128)(2,1)S(1)}, f32[32,128]{1,0:T(8,128)S(1)}, f32[32,384]{1,0:T(8,128)S(1)}) custom-call(bf16[32,1536]{1,0:T(8,128)(2,1)S(1)} %all_gather.6.qkv_ref, bf16[32,16,512]{2,1,0:T(8,128)(2,1)S(1)} %maximum_maximum_fusion.extra_ref, f32[32,384]{1,0:T(8,128)S(1)} %add_convert_fusion.mask_ref, ...), custom_call_target="tpu_custom_call" | custom-call | tf_op jit(solution)/shard_map/pallas_call | solution.py:123
  50.1 0.0 copy-done.2
  50.1 24.2 %shard_map.254 = (bf16[32,512]{1,0:T(8,128)(2,1)S(1)}, bf16[256,2048]{1,0:T(8,128)(2,1)S(1)}) custom-call(bf16[4,32,256]{2,1,0:T(8,128)(2,1)S(1)} %get-tuple-element.12.summed_ref, f32[32,128]{1,0:T(8,128)S(1)} %get-tuple-element.13.stats_ref, f32[32,384]{1,0:T(8,128)S(1)} %get-tuple-element.14.gated_ref, f32[1,384]{1,0:T(1,128)S(1)} %broadcast_in_dim.40.mixer_gain_ref, ...), custom_call_target="tpu_custom_call" | custom-call | tf_op jit(solution)/shard_map/pallas_call | solution.py:276
  74.3 0.0 copy-start.10
  74.3 0.0 copy-start.7
  74.3 0.0 copy-start.9
  74.3 6.7 %fusion.2 = bf16[32,8,2048]{2,1,0:T(8,128)(2,1)} fusion(bf16[256,2048]{1,0:T(8,128)(2,1)S(1)} %get-tuple-element.16, bf16[2048,2048]{1,0:T(8,128)(2,1)} %param.43), kind=kOutput, calls=%fused_computation.3 | convolution fusion | flops 2148007936 | bytes 10485760 | tf_op jit(solution)/shard_map/dot_general | solution.py:379
  81.1 4.0 %all-to-all-start = ((bf16[32,8,2048]{2,1,0:T(8,128)(2,1)}), bf16[32,8,2048]{2,1,0:T(8,128)(2,1)}, u32[]{:S(2)}, u32[]{:S(2)}) async-start(bf16[32,8,2048]{2,1,0:T(8,128)(2,1)} %fusion.2), calls=%async_computation | async-start | bytes 2097152 | tf_op jit(solution)/shard_map/all_to_all | solution.py:384
  85.1 0.6 slice.20
  85.7 0.6 fusion.19
  86.3 0.0 copy-done.9
  86.3 0.6 fusion.12
  87.0 24.3 %all-to-all-done = bf16[32,8,2048]{2,1,0:T(8,128)(2,1)} async-done(((bf16[32,8,2048]{2,1,0:T(8,128)(2,1)}), bf16[32,8,2048]{2,1,0:T(8,128)(2,1)}, u32[]{:S(2)}, u32[]{:S(2)}) %all-to-all-start) | async-done | bytes 1048608 | tf_op jit(solution)/shard_map/all_to_all | solution.py:384
  111.3 2.8 %convert_element_type.53 = f32[32,8,2048]{2,1,0:T(8,128)} convert(bf16[32,8,2048]{2,1,0:T(8,128)(2,1)} %all-to-all-done) | non-fusion elementwise | flops 524288 | bytes 3145728 | tf_op jit(solution)/shard_map/convert_element_type | solution.py:386
  114.1 0.6 copy.56
  (21 shorter events, 0.1 us)
Async XLA Ops:
  0.6 18.9 %copy-start = (bf16[2048,2,384]{2,1,0:T(2,128)(2,1)S(1)}, bf16[2048,2,384]{2,1,0:T(2,128)(2,1)}, u32[]{:S(2)}) copy-start(bf16[2048,2,384]{2,1,0:T(2,128)(2,1)} %param.25) | copy-start | bytes 9437188
  5.6 15.5 %copy-start.6 = (bf16[32,3,384]{2,0,1:T(8,128)(2,1)S(1)}, bf16[32,3,384]{2,0,1:T(8,128)(2,1)}, u32[]{:S(2)}) copy-start(bf16[32,3,384]{2,0,1:T(8,128)(2,1)} %param.31) | copy-start | bytes 221188
  21.2 0.6 copy-start.8
  32.8 2.8 %copy-start.1 = (bf16[32,6,64,256]{3,2,1,0:T(8,128)(2,1)S(1)}, bf16[32,6,64,256]{3,2,1,0:T(8,128)(2,1)}, u32[]{:S(2)}) copy-start(bf16[32,6,64,256]{3,2,1,0:T(8,128)(2,1)} %param.35) | copy-start | bytes 18874372
  35.6 14.5 %copy-start.2 = (bf16[32,2048]{1,0:T(8,128)(2,1)S(1)}, bf16[32,2048]{1,0:T(8,128)(2,1)}, u32[]{:S(2)}) copy-start(bf16[32,2048]{1,0:T(8,128)(2,1)} %residual_ref.1) | copy-start | bytes 393220
  35.6 14.5 %copy-start.3 = (bf16[384,2048]{1,0:T(8,128)(2,1)S(1)}, bf16[384,2048]{1,0:T(8,128)(2,1)}, u32[]{:S(2)}) copy-start(bf16[384,2048]{1,0:T(8,128)(2,1)} %mamba_out_ref.1) | copy-start | bytes 4718596
  35.6 14.5 %copy-start.4 = (bf16[256,2048]{1,0:T(8,128)(2,1)S(1)}, bf16[256,2048]{1,0:T(8,128)(2,1)}, u32[]{:S(2)}) copy-start(bf16[256,2048]{1,0:T(8,128)(2,1)} %attention_out_ref.1) | copy-start | bytes 3145732
  35.6 14.5 %copy-start.5 = (f32[2048]{0:T(1024)S(1)}, f32[2048]{0:T(1024)}, u32[]{:S(2)}) copy-start(f32[2048]{0:T(1024)} %param.42) | copy-start | bytes 24580
  74.3 11.4 %copy-start.10 = (bf16[32,3,128]{2,0,1:T(8,128)(2,1)S(1)}, bf16[32,3,128]{2,0,1:T(8,128)(2,1)}, u32[]{:S(2)}) copy-start(bf16[32,3,128]{2,0,1:T(8,128)(2,1)} %param.34) | copy-start | bytes 73732
  74.3 12.0 %copy-start.7 = (bf16[32,3,384]{2,0,1:T(8,128)(2,1)S(1)}, bf16[32,3,384]{2,0,1:T(8,128)(2,1)}, u32[]{:S(2)}) copy-start(bf16[32,3,384]{2,0,1:T(8,128)(2,1)} %param.31) | copy-start | bytes 221188
  74.3 12.0 %copy-start.9 = (bf16[32,1,384]{2,0,1:T(8,128)(2,1)S(1)}, bf16[32,1,384]{2,0,1:T(8,128)(2,1)}, u32[]{:S(2)}) copy-start(bf16[32,1,384]{2,0,1:T(8,128)(2,1)} %copy-done.8) | copy-start | bytes 73732
  81.1 30.3 %all-to-all-start = ((bf16[32,8,2048]{2,1,0:T(8,128)(2,1)}), bf16[32,8,2048]{2,1,0:T(8,128)(2,1)}, u32[]{:S(2)}, u32[]{:S(2)}) async-start(bf16[32,8,2048]{2,1,0:T(8,128)(2,1)} %fusion.2), calls=%async_computation | async-start | bytes 2097152 | tf_op jit(solution)/shard_map/all_to_all | solution.py:384

commit v2 on v1

--- a/solution.py
+++ b/solution.py
@@ -30,24 +30,128 @@
     return (widened * lax.rsqrt(mean_sq + EPSILON) * gain).astype(jnp.bfloat16)
 
 
-def conv_apply(old_state, fresh_row, taps):
-    window = jnp.concatenate([old_state, fresh_row[:, None, :]], axis=1)
-    mixed_rows = jnp.einsum("rkc,kc->rc", window, taps, preferred_element_type=jnp.float32)
-    return (jax.nn.silu(mixed_rows), window[:, 1:, :])
+def silu(v):
+    return v / (1.0 + jnp.exp(-v))
+
+
+def conv_rows(state_ref, fresh, taps_ref):
+    steps = [state_ref[k].astype(jnp.float32) for k in range(3)] + [fresh.astype(jnp.float32)]
+    taps = taps_ref[...].astype(jnp.float32)
+    mixed = steps[0] * taps[0:1]
+    for k in range(1, 4):
+        mixed = mixed + steps[k] * taps[k : k + 1]
+    return silu(mixed)
+
+
+def by_head(ref, g, shape):
+    lane = lax.broadcasted_iota(jnp.int32, shape, 1)
+    return jnp.where(lane < MP, ref[2 * g], ref[2 * g + 1])
+
+
+def entry_kernel(
+    tp_size, bias_ref, log_ref, residual_ref, gain_ref, attention_ref, coupling_ref, taps_ref,
+    state_ref, step_weight_ref, normed_ref, pre_ref, qkv_ref, coup_ref, step_ref, decay_ref,
+    qkv_s, qkv_r, coup_s, coup_r,
+):
+    r = lax.axis_index("req")
+    t = lax.axis_index("tp")
+    peers = [lax.rem(t + k, tp_size) for k in range(tp_size)]
+    barrier = pltpu.get_barrier_semaphore()
+    for k in range(1, tp_size):
+        pl.semaphore_signal(barrier, inc=1, device_id=(r, peers[k]), device_id_type=MESH)
+    normed = norm_rows(residual_ref[...], gain_ref[...])
+    normed_ref[...] = normed
+    copies = []
+
+    def share(out_ref, value, ssem, rsem):
+        width = value.shape[1]
+        cols = pl.ds(pl.multiple_of(t * width, 128), width)
+        out_ref[:, cols] = value
+        for k in range(1, tp_size):
+            copy = pltpu.make_async_remote_copy(
+                src_ref=out_ref.at[:, cols], dst_ref=out_ref.at[:, cols], send_sem=ssem.at[k],
+                recv_sem=rsem.at[k], device_id=(r, peers[k]), device_id_type=MESH,
+            )
+            copy.start()
+            copies.append(copy)
+
+    qkv = jnp.dot(normed, attention_ref[...], preferred_element_type=jnp.float32)
+    pl.semaphore_wait(barrier, tp_size - 1)
+    share(qkv_ref, qkv.astype(jnp.bfloat16), qkv_s, qkv_r)
+    pre = jnp.dot(normed, coupling_ref[...], preferred_element_type=jnp.float32).astype(jnp.bfloat16)
+    pre_ref[...] = pre
+    share(coup_ref, conv_rows(state_ref, pre, taps_ref).astype(jnp.bfloat16), coup_s, coup_r)
+    steps = (
+        lax.dot_general(normed, step_weight_ref[...], NT, preferred_element_type=jnp.float32)
+        .astype(jnp.bfloat16)
+        .astype(jnp.float32)
+    )
+    shape = (normed.shape[0], 2 * MP)
+    for g in range(steps.shape[1] // 2):
+        lane = lax.broadcasted_iota(jnp.int32, shape, 1)
+        v = jnp.where(lane < MP, steps[:, 2 * g : 2 * g + 1], steps[:, 2 * g + 1 : 2 * g + 2])
+        v = v + by_head(bias_ref, g, shape)
+        size = jnp.maximum(v, 0.0) + jnp.log1p(jnp.exp(-jnp.abs(v)))
+        step_ref[:, g * 2 * MP : (g + 1) * 2 * MP] = size
+        decay_ref[:, g * 2 * MP : (g + 1) * 2 * MP] = jnp.exp(
+            -size * jnp.exp(by_head(log_ref, g, shape))
+        )
+    for copy in copies:
+        copy.wait()
+
+
+def entry(bias, decay_log, residual, gain, attention_weight, coupling_weight, taps, state, step_weight):
+    tp_size = lax.axis_size("tp")
+    rows, model = residual.shape
+    units = bias.shape[0] * MP
+    vmem = pl.BlockSpec(memory_space=pltpu.VMEM)
+    smem = pl.BlockSpec(memory_space=pltpu.SMEM)
+    dma = pltpu.SemaphoreType.DMA((tp_size,))
+    shaped = jax.ShapeDtypeStruct
+    return pl.pallas_call(
+        functools.partial(entry_kernel, tp_size),
+        in_specs=[smem] * 2 + [vmem] * 7,
+        out_specs=[vmem] * 6,
+        out_shape=[
+            shaped((rows, model), jnp.bfloat16),
+            shaped((rows, coupling_weight.shape[1]), jnp.bfloat16),
+            shaped((rows, attention_weight.shape[1] * tp_size), jnp.bfloat16),
+            shaped((rows, coupling_weight.shape[1] * tp_size), jnp.bfloat16),
+            shaped((rows, units), jnp.float32),
+            shaped((rows, units), jnp.float32),
+        ],
+        scratch_shapes=[dma] * 4,
+        compiler_params=pltpu.CompilerParams(
+            collective_id=0, has_side_effects=True, vmem_limit_bytes=16 << 20
+        ),
+    )(bias, decay_log, residual, gain[None], attention_weight, coupling_weight, taps, state, step_weight)
 
 
 def mixer_kernel(
-    qkv_ref, extra_ref, mask_ref, window_ref, state_ref, coup_ref, x_ref, step_ref, decay_ref,
-    gate_ref, skip_ref, new_state_ref, summed_ref, stats_ref, gated_ref, heads_scr,
+    len_ref, skip_ref, qkv_ref, sink_ref, window_ref, state_ref, coup_ref, pre_ref, coup_state_ref,
+    projected_ref, taps_ref, conv_state_ref, step_ref, decay_ref, new_state_ref, new_conv_ref,
+    new_coup_ref, summed_ref, stats_ref, gated_ref, heads_scr, extra_scr,
 ):
     half = KVH * HD
     group = QH // KVH
+    t = lax.axis_index("tp")
     for h in range(QH):
         heads_scr[pl.ds(h, BR, stride=QH), :] = qkv_ref[:, h * HD : (h + 1) * HD].astype(jnp.float32)
+    extra_scr[...] = jnp.zeros_like(extra_scr)
+    fresh_rows = qkv_ref[:, QH * HD :].astype(jnp.float32)
+    units = step_ref.shape[1]
+    gate = projected_ref[0].astype(jnp.float32)
+    x_pre = projected_ref[1]
+    x = conv_rows(conv_state_ref, x_pre, taps_ref)
+    new_conv_ref[0] = conv_state_ref[1]
+    new_conv_ref[1] = conv_state_ref[2]
+    new_conv_ref[2] = x_pre
+    new_coup_ref[0] = coup_state_ref[1]
+    new_coup_ref[1] = coup_state_ref[2]
+    new_coup_ref[2] = pre_ref[...]
     head_row = lax.broadcasted_iota(jnp.int32, (QH, HD), 0)
     lane = lax.broadcasted_iota(jnp.int32, (QH, HD), 1)
     first_half = head_row < group
-    x = x_ref[...]
     step_x = step_ref[...] * x
     decay = decay_ref[...]
     step_x_t = step_x.T
@@ -62,15 +166,21 @@
         wide = jnp.concatenate(
             [jnp.where(first_half, q, 0.0), jnp.where(first_half, 0.0, q)], axis=1
         ).astype(jnp.bfloat16)
+        extra_scr[j, :SINK, :] = sink_ref[j].astype(jnp.float32)
+        extra_scr[j, SINK : SINK + 1, :] = fresh_rows[j : j + 1, :]
+        extra = extra_scr[j].astype(jnp.bfloat16)
         s1 = lax.dot_general(
             wide, window_ref[j, :, :half], NT, preferred_element_type=jnp.float32
         ) * HD ** (-0.5)
         s2 = lax.dot_general(
-            wide, extra_ref[j, :, :half], NT, preferred_element_type=jnp.float32
+            wide, extra[:, :half], NT, preferred_element_type=jnp.float32
         ) * HD ** (-0.5)
+        last = len_ref[pl.program_id(0) * BR + j] - 1
         slots = window_ref.shape[1]
-        live1 = jnp.broadcast_to(mask_ref[j : j + 1, :slots], s1.shape) > 0.5
-        live2 = jnp.broadcast_to(mask_ref[j : j + 1, slots : slots + EXTRA], s2.shape) > 0.5
+        slot = t * slots + lax.broadcasted_iota(jnp.int32, s1.shape, 1)
+        back = jnp.bitwise_and(last - slot, WIN - 1)
+        live1 = (last - back >= SINK) & (back != WIN - 1)
+        live2 = lax.broadcasted_iota(jnp.int32, s2.shape, 1) < jnp.where(t == 0, SINK + 1, 0)
         s1 = jnp.where(live1, s1, NEG_BIG)
         s2 = jnp.where(live2, s2, NEG_BIG)
         peak = jnp.maximum(
@@ -82,7 +192,7 @@
         acc = jnp.dot(
             w1.astype(jnp.bfloat16), window_ref[j, :, half:], preferred_element_type=jnp.float32
         ) + jnp.dot(
-            w2.astype(jnp.bfloat16), extra_ref[j, :, half:], preferred_element_type=jnp.float32
+            w2.astype(jnp.bfloat16), extra[:, half:], preferred_element_type=jnp.float32
         )
         heads_scr[j * QH : (j + 1) * QH, :] = jnp.where(first_half, acc[:, :HD], acc[:, HD:])
         stats_ref[j : j + 1, :] = jnp.sum(
@@ -104,9 +214,11 @@
         summed_ref[h // per_chunk, :, (h % per_chunk) * HD : (h % per_chunk + 1) * HD] = heads_scr[
             pl.ds(h, BR, stride=QH), :
         ].astype(jnp.bfloat16)
-    readout = decay * jnp.concatenate(read_rows, axis=0) + step_x * both + skip_ref[...] * x
-    gate = gate_ref[...].astype(jnp.float32)
-    gated = readout * (gate / (1.0 + jnp.exp(-gate)))
+    readout = decay * jnp.concatenate(read_rows, axis=0) + step_x * both
+    skip = jnp.concatenate(
+        [by_head(skip_ref, g, (BR, 2 * MP)) for g in range(units // (2 * MP))], axis=1
+    )
+    gated = (readout + skip * x) * silu(gate)
     gated_ref[...] = gated
     square = jnp.sum(gated * gated, axis=1, keepdims=True)
     stats_ref[...] = jnp.where(
@@ -114,32 +226,46 @@
     )
 
 
-def mixer(qkv, extra, mask, window, state, coup, x, step, decay, gate, skip, tp_size):
-    rows, units = x.shape
-    slots = window.shape[1]
-    row = lambda width: pl.BlockSpec((BR, width), lambda i: (i, 0))
+def mixer(
+    lengths, skip, qkv, sink, window, state, coup, pre, coup_state, projected, taps, conv_state,
+    step, decay, tp_size,
+):
+    rows, units = step.shape
+    row = lambda a: pl.BlockSpec((BR, a.shape[1]), lambda i: (i, 0))
     cube = lambda a: pl.BlockSpec((BR,) + a.shape[1:], lambda i: (i, 0, 0))
+    steps = lambda a: pl.BlockSpec((3, BR, a.shape[2]), lambda i: (0, i, 0))
+    smem = pl.BlockSpec(memory_space=pltpu.SMEM)
     chunk = QH * HD // tp_size
     return pl.pallas_call(
         mixer_kernel,
         grid=(rows // BR,),
         in_specs=[
-            row(qkv.shape[1]), cube(extra), row(mask.shape[1]), cube(window), cube(state),
-            row(coup.shape[1]), row(units), row(units), row(units), row(units),
-            pl.BlockSpec((1, units), lambda i: (0, 0)),
+            smem, smem, row(qkv), cube(sink), cube(window), cube(state), row(coup), row(pre),
+            steps(coup_state), pl.BlockSpec((2, BR, units), lambda i: (0, i, 0)), pl.BlockSpec(taps.shape, lambda i: (0, 0)),
+            steps(conv_state), row(step), row(decay),
         ],
         out_specs=[
-            cube(state), pl.BlockSpec((tp_size, BR, chunk), lambda i: (0, i, 0)), row(128), row(units),
+            cube(state), steps(conv_state), steps(coup_state),
+            pl.BlockSpec((tp_size, BR, chunk), lambda i: (0, i, 0)),
+            pl.BlockSpec((BR, 128), lambda i: (i, 0)), row(step),
         ],
         out_shape=[
             jax.ShapeDtypeStruct(state.shape, jnp.bfloat16),
+            jax.ShapeDtypeStruct(conv_state.shape, jnp.bfloat16),
+            jax.ShapeDtypeStruct(coup_state.shape, jnp.bfloat16),
             jax.ShapeDtypeStruct((tp_size, rows, chunk), jnp.bfloat16),
             jax.ShapeDtypeStruct((rows, 128), jnp.float32),
             jax.ShapeDtypeStruct((rows, units), jnp.float32),
         ],
-        scratch_shapes=[pltpu.VMEM((BR * QH, HD), jnp.float32)],
+        scratch_shapes=[
+            pltpu.VMEM((BR * QH, HD), jnp.float32),
+            pltpu.VMEM((BR, EXTRA, 2 * KVH * HD), jnp.float32),
+        ],
         compiler_params=pltpu.CompilerParams(vmem_limit_bytes=40 << 20),
-    )(qkv, extra, mask, window, state, coup, x, step, decay, gate, skip)
+    )(
+        lengths, skip, qkv, sink, window, state, coup, pre, coup_state, projected, taps, conv_state,
+        step, decay,
+    )
 
 
 def joint_kernel(
@@ -322,56 +448,24 @@
 ):
     row_count = residual.shape[0]
     tp_size = lax.axis_size("tp")
-    tp_index = lax.axis_index("tp")
     local_units = inner_weight.shape[2]
-    half_width = KVH * HD
-    normed = norm_rows(residual, input_gain)
+    swap = lambda array: jnp.transpose(array, (1, 0, 2))
+    coup_state = swap(coupling_state)
+    normed, coupling_pre, qkv_rows, coupling_all, step_size, decay_rate = entry(
+        step_bias, decay_log, residual, input_gain, attention_weight, coupling_weight,
+        coupling_conv, coup_state, step_weight.T,
+    )
     projected = jnp.einsum(
-        "rd,dtc->rtc", normed, inner_weight, preferred_element_type=jnp.float32
+        "rd,dtc->trc", normed, inner_weight, preferred_element_type=jnp.float32
     ).astype(jnp.bfloat16)
-    gate_rows = lax.optimization_barrier(projected[:, 0, :])
-    x_rows, new_conv_state = conv_apply(conv_state, projected[:, 1, :], conv_weight)
-    step_rows = lax.optimization_barrier(
-        jnp.dot(normed, step_weight, preferred_element_type=jnp.float32).astype(jnp.bfloat16)
-    )
-    step_size = jax.nn.softplus(step_rows.astype(jnp.float32) + step_bias)
-    decay_rate = jnp.exp(-step_size * jnp.exp(decay_log))
-    coupling_pre = jnp.dot(normed, coupling_weight, preferred_element_type=jnp.float32).astype(
-        jnp.bfloat16
-    )
-    coupling_rows, new_coupling_state = conv_apply(coupling_state, coupling_pre, coupling_conv)
-    qkv_local = jnp.dot(normed, attention_weight, preferred_element_type=jnp.float32).astype(
-        jnp.bfloat16
-    )
-    qkv_rows, coupling_all = (
-        lax.all_gather(qkv_local, "tp", axis=1, tiled=True),
-        lax.all_gather(coupling_rows.astype(jnp.bfloat16), "tp", axis=1, tiled=True),
-    )
     new_key_value = qkv_rows[:, QH * HD :]
-    window_slots = window_cache.shape[1]
-    slot_index = tp_index * window_slots + jnp.arange(window_slots, dtype=jnp.int32)
-    length_column = cache_lengths[:, None]
-    back_steps = (length_column - 1 - slot_index[None, :]) % WIN
-    position = length_column - 1 - back_steps
-    live_mask = (position >= SINK) & (back_steps != WIN - 1)
-    extra_live = (jnp.arange(128) < SINK + 1) & (tp_index == 0)
-    mask = jnp.concatenate(
-        [live_mask, jnp.broadcast_to(extra_live, (row_count, 128))], axis=1
-    ).astype(jnp.float32)
-    extra = jnp.concatenate(
-        [
-            sink_cache,
-            new_key_value[:, None, :],
-            jnp.zeros((row_count, EXTRA - SINK - 1, 2 * half_width), jnp.bfloat16),
-        ],
-        axis=1,
-    )
-    spread = lambda per_head: jnp.repeat(per_head, MP, axis=-1)
-    new_state, summed, stats, gated = mixer(
-        qkv_rows, extra, mask, window_cache, scan_state.reshape(row_count, local_units, NS),
-        coupling_all, x_rows, spread(step_size), spread(decay_rate), gate_rows,
-        spread(skip_gain)[None], tp_size,
-    )
+    new_state, new_conv, new_coup, summed, stats, gated = mixer(
+        cache_lengths, skip_gain, qkv_rows, sink_cache, window_cache,
+        scan_state.reshape(row_count, local_units, NS), coupling_all, coupling_pre, coup_state,
+        projected, conv_weight, swap(conv_state), step_size, decay_rate, tp_size,
+    )
+    new_conv_state = swap(new_conv)
+    new_coupling_state = swap(new_coup)
     new_scan_state = new_state.reshape(scan_state.shape)
     new_residual, final_rows = joint(
         summed, stats, gated, mixer_gain, mamba_out, attention_out, residual, final_gain

time: 115 us -> 95.2 us (0.83)
  blocking collectives: 11.7 us -> 0 us
  matrix products: 12.8 us -> 3.96 us
  other arithmetic: 10.8 us -> 2.79 us
  Pallas kernels: 38.6 us -> 44.7 us
  waiting for transfers between devices: 24.3 us -> 25.6 us
    all_gather x2 -> x0, blocking collectives: 11.7 us -> none  [the longest x1 6.08 us: body(): lax.all_gather(coupling_rows.astype(jnp.bfloat16), 'tp', axis=1, tiled=True)]
    unnamed x23 -> x45, local copies, waits for them, and re-layouts: 4 us -> 11.1 us
    pallas_call x1 -> x2, Pallas kernels: 14.4 us -> 20.8 us  [the longest x1 14.5 us: mixer(): pl.pallas_call(mixer_kernel, grid=(rows // BR,), in_specs=[smem, smem, ro...]
    dot_general x4 -> x1, matrix products: 6.02 us -> 0.65 us  [body(): jnp.einsum('rd,dtc->trc', normed, inner_weight, preferred_element_type=jn...]
    dot_general x1, matrix products: 6.74 us -> 3.3 us  [body(): jnp.dot(final_rows, output_head, preferred_element_type=jnp.float32)]
    broadcast_in_dim x6 -> x0, local copies, waits for them, and re-layouts: 2.97 us -> none  [the longest x3 2.29 us: body(): spread = lambda per_head: jnp.repeat(per_head, MP, axis=-1)]
    concatenate x3 -> x0, other arithmetic: 2.44 us -> none  [the longest x2 1.26 us: conv_apply(): window = jnp.concatenate([old_state, fresh_row[:, None, :]], axis=1)]
    unnamed x2 -> x0, other arithmetic: 1.41 us -> none
  transfers between devices with their start and end apart: 1 -> 1, of which waited for: 1 -> 1; matrix products, arithmetic and copies ran while one was open for 2% -> 1% of each run, Pallas kernels for 0% -> 0%
where the time goes in v2:
time: 95.2 us; the launch traced here: 94.6 us
  Pallas kernels  44.7 us (47%)
  waiting for transfers between devices  25.6 us (27%)
  local copies, waits for them, and re-layouts  12.6 us (13%)
  starting transfers between devices  4.21 us (4%)
  matrix products  3.96 us (4%)
  other arithmetic  2.79 us (3%)
    all_to_all x1, waiting for transfers between devices, body(): lax.all_to_all(vocab_logits.astype(jnp.bfloat16), ('req', 'tp'), split_ax...  25.6 us
    pallas_call x1, Pallas kernels, joint(): pl.pallas_call(functools.partial(joint_kernel, tp_size, req_size), in_spe...  23.9 us
    pallas_call x1, Pallas kernels, mixer(): pl.pallas_call(mixer_kernel, grid=(rows // BR,), in_specs=[smem, smem, ro...  14.5 us
    unnamed x45, local copies, waits for them, and re-layouts  11.1 us
    pallas_call x1, Pallas kernels, entry(): pl.pallas_call(functools.partial(entry_kernel, tp_size), in_specs=[smem]...  6.32 us
    all_to_all x1, starting transfers between devices, body(): lax.all_to_all(vocab_logits.astype(jnp.bfloat16), ('req', 'tp'), split_ax...  4.21 us
    dot_general x1, matrix products, body(): jnp.dot(final_rows, output_head, preferred_element_type=jnp.float32)  3.3 us
    convert_element_type x1, other arithmetic, body(): logits = lax.all_to_all(vocab_logits.astype(jnp.bfloat16), ('req', 'tp'),...  2.79 us
  transfers between devices with their start and end apart: 1, of which 1 were waited for; matrix products, arithmetic and copies ran while one was open for 1% of the time, Pallas kernels for 0%

profile of v2, /device:TPU:0, one launch (start us, length us, event | category | flops | bytes accessed | tf_op | source)
XLA Modules:
  0.0 94.6 jit_solution(5471573310508916970)
XLA Ops:
  0.6 0.0 copy-start
  0.6 0.0 copy-start.15
  0.7 0.0 copy-start.18
  0.7 0.0 copy-start.17
  0.7 0.8 broadcast_in_dim.10.mixer_gain_ref
  1.5 0.0 copy-start.3
  1.5 1.5 %copy-done.3 = bf16[2048,384]{1,0:T(8,128)(2,1)S(1)} copy-done((bf16[2048,384]{1,0:T(8,128)(2,1)S(1)}, bf16[2048,384]{1,0:T(8,128)(2,1)}, u32[]{:S(2)}) %copy-start.3) | copy-done | bytes 1572888
  3.1 0.0 copy-start.5
  3.1 1.0 %copy-done.5 = bf16[2048,128]{1,0:T(8,128)(2,1)S(1)} copy-done((bf16[2048,128]{1,0:T(8,128)(2,1)S(1)}, bf16[2048,128]{1,0:T(8,128)(2,1)}, u32[]{:S(2)}) %copy-start.5) | copy-done | bytes 524312
  4.1 0.0 copy-start.6
  4.1 0.9 copy-done.6
  5.0 0.0 copy-start.9
  5.0 0.7 copy-done.9
  5.7 0.0 copy-start.12
  5.7 0.8 copy-done.12
  6.5 0.0 copy-start.13
  6.5 0.7 copy-done.13
  7.2 0.0 copy-start.16
  7.2 0.7 copy-done.16
  7.9 0.0 copy-start.19
  7.9 0.7 copy-done.19
  8.5 0.0 copy-start.20
  8.5 0.7 copy-done.20
  9.2 6.3 %shard_map.253 = (bf16[32,2048]{1,0:T(8,128)(2,1)S(1)}, bf16[32,128]{1,0:T(8,128)(2,1)S(1)}, bf16[32,1536]{1,0:T(8,128)(2,1)S(1)}, bf16[32,512]{1,0:T(8,128)(2,1...) custom-call(f32[6]{0:T(128)S(1)} %copy-done.19, f32[6]{0:T(128)S(1)} %copy-done.20, bf16[32,2048]{1,0:T(8,128)(2,1)S(1)} %copy-done.6, ...), custom_call_target="tpu_custom_call" | custom-call | tf_op jit(solution)/shard_map/pallas_call | solution.py:111
  15.5 0.0 copy-done
  15.5 0.7 fusion.6.projected_ref
  16.2 0.0 copy-done.15
  16.2 0.0 copy-done.18
  16.2 0.0 copy-done.17
  16.2 0.0 copy-done.8
  16.2 0.0 copy-done.10
  16.2 0.0 copy-done.11
  16.3 0.0 copy-start.1
  16.3 2.8 %copy-done.1 = bf16[32,6,64,256]{3,2,1,0:T(8,128)(2,1)S(1)} copy-done((bf16[32,6,64,256]{3,2,1,0:T(8,128)(2,1)S(1)}, bf16[32,6,64,256]{3,2,1,0:T(8,128)(2,1)}, u32[]{:S(2)}) %copy-start.1) | copy-done | bytes 6291480
  19.1 0.0 copy-start.21
  19.1 14.5 %shard_map.254 = (bf16[32,384,256]{2,1,0:T(8,128)(2,1)}, bf16[3,32,384]{2,1,0:T(8,128)(2,1)}, bf16[3,32,128]{2,1,0:T(8,128)(2,1)}, bf16[4,32,256]{2,1,0:T(8,128)...) custom-call(s32[32]{0:T(128)S(1)} %copy-done.17, f32[6]{0:T(128)S(1)} %copy-done.18, ...), custom_call_target="tpu_custom_call" | custom-call | tf_op jit(solution)/shard_map/pallas_call | solution.py:239
  33.5 0.0 copy-done.2
  33.5 0.0 copy-done.4
  33.5 0.0 copy-done.7
  33.6 0.0 copy-done.14
  33.6 23.9 %shard_map.255 = (bf16[32,512]{1,0:T(8,128)(2,1)S(1)}, bf16[256,2048]{1,0:T(8,128)(2,1)S(1)}) custom-call(bf16[4,32,256]{2,1,0:T(8,128)(2,1)S(1)} %get-tuple-element.26.summed_ref, f32[32,128]{1,0:T(8,128)S(1)} %get-tuple-element.27.stats_ref, f32[32,384]{1,0:T(8,128)S(1)} %get-tuple-element.28.gated_ref, f32[1,384]{1,0:T(1,128)S(1)} %broadcast_in_dim.10.mixer_gain_ref, ...), custom_call_target="tpu_custom_call" | custom-call | tf_op jit(solution)/shard_map/pallas_call | solution.py:402
  57.5 0.0 copy-done.21
  57.5 3.3 %fusion.2 = bf16[32,8,2048]{2,1,0:T(8,128)(2,1)} fusion(bf16[256,2048]{1,0:T(8,128)(2,1)S(1)} %get-tuple-element.30, bf16[2048,2048]{1,0:T(8,128)(2,1)S(1)} %copy-done.21), kind=kOutput, calls=%fused_computation.3 | convolution fusion | flops 2148007936 | bytes 10485760 | tf_op jit(solution)/shard_map/dot_general | solution.py:473
  60.8 4.2 %all-to-all-start = ((bf16[32,8,2048]{2,1,0:T(8,128)(2,1)}), bf16[32,8,2048]{2,1,0:T(8,128)(2,1)}, u32[]{:S(2)}, u32[]{:S(2)}) async-start(bf16[32,8,2048]{2,1,0:T(8,128)(2,1)} %fusion.2), calls=%async_computation | async-start | bytes 2097152 | tf_op jit(solution)/shard_map/all_to_all | solution.py:478
  65.0 0.6 slice.3
  65.6 25.6 %all-to-all-done = bf16[32,8,2048]{2,1,0:T(8,128)(2,1)} async-done(((bf16[32,8,2048]{2,1,0:T(8,128)(2,1)}), bf16[32,8,2048]{2,1,0:T(8,128)(2,1)}, u32[]{:S(2)}, u32[]{:S(2)}) %all-to-all-start) | async-done | bytes 1048608 | tf_op jit(solution)/shard_map/all_to_all | solution.py:478
  91.2 2.8 %convert_element_type.24 = f32[32,8,2048]{2,1,0:T(8,128)} convert(bf16[32,8,2048]{2,1,0:T(8,128)(2,1)} %all-to-all-done) | non-fusion elementwise | flops 524288 | bytes 3145728 | tf_op jit(solution)/shard_map/convert_element_type | solution.py:480
  94.0 0.6 copy.36
  (7 shorter events, 0.0 us)
Async XLA Ops:
  0.6 14.9 %copy-start = (bf16[2048,2,384]{2,1,0:T(2,128)(2,1)S(1)}, bf16[2048,2,384]{2,1,0:T(2,128)(2,1)}, u32[]{:S(2)}) copy-start(bf16[2048,2,384]{2,1,0:T(2,128)(2,1)} %param.25) | copy-start | bytes 9437188
  0.6 15.5 %copy-start.15 = (bf16[4,384]{1,0:T(4,128)(2,1)S(1)}, bf16[4,384]{1,0:T(4,128)(2,1)}, u32[]{:S(2)}) copy-start(bf16[4,384]{1,0:T(4,128)(2,1)} %taps_ref.3) | copy-start | bytes 9220
  0.7 15.5 %copy-start.18 = (f32[6]{0:T(128)S(1)}, f32[6]{0:T(128)}, u32[]{:S(2)}) copy-start(f32[6]{0:T(128)} %skip_ref.1) | copy-start | bytes 76
  0.7 15.5 %copy-start.17 = (s32[32]{0:T(128)S(1)}, s32[32]{0:T(128)}, u32[]{:S(2)}) copy-start(s32[32]{0:T(128)} %len_ref.1) | copy-start | bytes 388
  1.5 1.5 %copy-start.3 = (bf16[2048,384]{1,0:T(8,128)(2,1)S(1)}, bf16[2048,384]{1,0:T(8,128)(2,1)}, u32[]{:S(2)}) copy-start(bf16[2048,384]{1,0:T(8,128)(2,1)} %attention_ref.1) | copy-start | bytes 4718596
  3.1 1.0 %copy-start.5 = (bf16[2048,128]{1,0:T(8,128)(2,1)S(1)}, bf16[2048,128]{1,0:T(8,128)(2,1)}, u32[]{:S(2)}) copy-start(bf16[2048,128]{1,0:T(8,128)(2,1)} %coupling_ref.1) | copy-start | bytes 1572868
  4.1 0.9 copy-start.6
  5.0 0.7 copy-start.9
  5.7 0.8 copy-start.12
  6.5 0.7 copy-start.13
  7.2 0.7 copy-start.16
  7.9 0.7 copy-start.19
  8.5 0.7 copy-start.20
  9.2 7.0 %copy-start.8 = (bf16[32,4,512]{2,1,0:T(4,128)(2,1)S(1)}, bf16[32,4,512]{2,1,0:T(4,128)(2,1)}, u32[]{:S(2)}) copy-start(bf16[32,4,512]{2,1,0:T(4,128)(2,1)} %sink_ref.1) | copy-start | bytes 393220
  9.2 7.0 %copy-start.10 = (bf16[32,3,128]{2,0,1:T(8,128)(2,1)S(1)}, bf16[32,3,128]{2,0,1:T(8,128)(2,1)}, u32[]{:S(2)}) copy-start(bf16[32,3,128]{2,0,1:T(8,128)(2,1)} %param.34) | copy-start | bytes 73732
  9.2 7.1 %copy-start.11 = (bf16[32,3,384]{2,0,1:T(8,128)(2,1)S(1)}, bf16[32,3,384]{2,0,1:T(8,128)(2,1)}, u32[]{:S(2)}) copy-start(bf16[32,3,384]{2,0,1:T(8,128)(2,1)} %param.31) | copy-start | bytes 221188
  16.3 2.8 %copy-start.1 = (bf16[32,6,64,256]{3,2,1,0:T(8,128)(2,1)S(1)}, bf16[32,6,64,256]{3,2,1,0:T(8,128)(2,1)}, u32[]{:S(2)}) copy-start(bf16[32,6,64,256]{3,2,1,0:T(8,128)(2,1)} %param.35) | copy-start | bytes 18874372
  19.0 14.5 %copy-start.2 = (bf16[384,2048]{1,0:T(8,128)(2,1)S(1)}, bf16[384,2048]{1,0:T(8,128)(2,1)}, u32[]{:S(2)}) copy-start(bf16[384,2048]{1,0:T(8,128)(2,1)} %mamba_out_ref.1) | copy-start | bytes 4718596
  19.0 14.5 %copy-start.4 = (bf16[256,2048]{1,0:T(8,128)(2,1)S(1)}, bf16[256,2048]{1,0:T(8,128)(2,1)}, u32[]{:S(2)}) copy-start(bf16[256,2048]{1,0:T(8,128)(2,1)} %attention_out_ref.1) | copy-start | bytes 3145732
  19.0 14.5 %copy-start.7 = (bf16[32,2048]{1,0:T(8,128)(2,1)S(1)}, bf16[32,2048]{1,0:T(8,128)(2,1)}, u32[]{:S(2)}) copy-start(bf16[32,2048]{1,0:T(8,128)(2,1)} %residual_ref.3) | copy-start | bytes 393220
  19.0 14.5 %copy-start.14 = (f32[2048]{0:T(1024)S(1)}, f32[2048]{0:T(1024)}, u32[]{:S(2)}) copy-start(f32[2048]{0:T(1024)} %param.42) | copy-start | bytes 24580
  19.1 38.4 %copy-start.21 = (bf16[2048,2048]{1,0:T(8,128)(2,1)S(1)}, bf16[2048,2048]{1,0:T(8,128)(2,1)}, u32[]{:S(2)}) copy-start(bf16[2048,2048]{1,0:T(8,128)(2,1)} %param.43) | copy-start | bytes 25165828
  60.8 30.4 %all-to-all-start = ((bf16[32,8,2048]{2,1,0:T(8,128)(2,1)}), bf16[32,8,2048]{2,1,0:T(8,128)(2,1)}, u32[]{:S(2)}, u32[]{:S(2)}) async-start(bf16[32,8,2048]{2,1,0:T(8,128)(2,1)} %fusion.2), calls=%async_computation | async-start | bytes 2097152 | tf_op jit(solution)/shard_map/all_to_all | solution.py:478

commit v3 on v2

--- a/solution.py
+++ b/solution.py
@@ -270,9 +270,9 @@
 
 def joint_kernel(
     tp_size, req_size, summed_ref, stats_ref, gated_ref, mixer_gain_ref, mamba_out_ref,
-    attention_out_ref, residual_ref, final_gain_ref, new_residual_ref, final_ref,
-    sum_buf, stat_buf, part_out, part_buf, gather, sum_s, sum_r, stat_s, stat_r, part_s, part_r,
-    gat_s, gat_r,
+    attention_out_ref, residual_ref, final_gain_ref, head_ref, new_residual_ref, logits_ref,
+    sum_buf, stat_buf, part_out, part_buf, gather, final_buf, head_buf, logit_out, logit_buf,
+    sum_s, sum_r, stat_s, stat_r, part_s, part_r, gat_s, gat_r, log_s, log_r, head_sem,
 ):
     r = lax.axis_index("req")
     t = lax.axis_index("tp")
@@ -281,11 +281,15 @@
     peers = [lax.rem(t + k, tp_size) for k in range(tp_size)]
     reqs = [lax.rem(r + k, req_size) for k in range(req_size)]
     barrier = pltpu.get_barrier_semaphore()
-    for k in range(1, tp_size):
-        pl.semaphore_signal(barrier, inc=1, device_id=(r, peers[k]), device_id_type=MESH)
-    for k in range(1, req_size):
-        pl.semaphore_signal(barrier, inc=1, device_id=(reqs[k], t), device_id_type=MESH)
-    pl.semaphore_wait(barrier, tp_size - 1 + req_size - 1)
+    load_head = pltpu.make_async_copy(head_ref, head_buf, head_sem.at[0])
+    load_head.start()
+    for k in range(req_size):
+        for q in range(tp_size):
+            if k or q:
+                pl.semaphore_signal(
+                    barrier, inc=1, device_id=(reqs[k], peers[q]), device_id_type=MESH
+                )
+    pl.semaphore_wait(barrier, tp_size * req_size - 1)
 
     def send(src, dst, ssem, rsem, where):
         copy = pltpu.make_async_remote_copy(
@@ -378,11 +382,54 @@
             jnp.add, [jnp.sum(v * v, axis=1, keepdims=True) for v in values]
         ) / (width * tp_size)
         scale = lax.rsqrt(mean + EPSILON)
-        source = lax.rem(r + req_size - k, req_size)
-        at = pl.ds(pl.multiple_of(source * rows, rows), rows)
         for i in range(4):
             cols = pl.ds(pl.multiple_of(owner[i] * width, 128), width)
-            final_ref[at, cols] = (values[i] * scale * final_gain_ref[:, cols]).astype(jnp.bfloat16)
+            final_buf[k * rows : (k + 1) * rows, cols] = (
+                values[i] * scale * final_gain_ref[:, cols]
+            ).astype(jnp.bfloat16)
+    load_head.wait()
+    vocab = head_buf.shape[1]
+    tile = min(512, vocab)
+    each = rows // tp_size
+    pairs = list(range(0, req_size, 2))
+    pairs = sorted(pairs, key=lambda k: abs(k + 0.5 - req_size / 2))
+    sent = []
+    for first_k in pairs:
+
+        def head_tile(c, carry, first_k=first_k):
+            cols = pl.ds(pl.multiple_of(c * tile, 128), tile)
+            part = jnp.dot(
+                final_buf[first_k * rows : (first_k + 2) * rows, :], head_buf[:, cols],
+                preferred_element_type=jnp.float32,
+            ).astype(jnp.bfloat16)
+            for i in range(2):
+                for q in range(tp_size):
+                    at = i * rows + q * each
+                    logit_out[first_k + i, q, :, cols] = part[at : at + each, :]
+            return carry
+
+        lax.fori_loop(0, vocab // tile, head_tile, 0)
+        for k in (first_k, first_k + 1):
+            back = lax.rem(r + req_size - k, req_size)
+            for q in range(tp_size):
+                if k or q:
+                    copy = send(
+                        logit_out.at[k, peers[q]], logit_buf.at[k, q], log_s.at[k, q],
+                        log_r.at[k, q], (back, peers[q]),
+                    )
+                    sent.append((k, q, copy))
+
+    def place(value, k, q):
+        source = reqs[k] * tp_size + lax.rem(t + tp_size - q, tp_size)
+        cols = pl.ds(pl.multiple_of(source * vocab, 128), vocab)
+        logits_ref[:, cols] = value.astype(jnp.float32)
+
+    place(logit_out[0, t], 0, 0)
+    for k, q, copy in sorted(sent, key=lambda item: min(item[0], req_size - item[0])):
+        copy.wait_recv()
+        place(logit_buf[k, q], k, q)
+    for k, q, copy in sent:
+        copy.wait_send()
     for k in range(req_size):
         if k:
             along[k].wait_send()
@@ -391,21 +438,25 @@
         far[k].wait_send()
 
 
-def joint(summed, stats, gated, mixer_gain, mamba_out, attention_out, residual, final_gain):
+def joint(
+    summed, stats, gated, mixer_gain, mamba_out, attention_out, residual, final_gain, output_head
+):
     tp_size = lax.axis_size("tp")
     req_size = lax.axis_size("req")
     rows, model = residual.shape
     width = model // tp_size
     chunk = summed.shape[2]
+    each = rows // tp_size
+    vocab = output_head.shape[1]
     dma = lambda *shape: pltpu.SemaphoreType.DMA(shape)
     vmem = pl.BlockSpec(memory_space=pltpu.VMEM)
     return pl.pallas_call(
         functools.partial(joint_kernel, tp_size, req_size),
-        in_specs=[vmem] * 8,
+        in_specs=[vmem] * 8 + [pl.BlockSpec(memory_space=pl.ANY)],
         out_specs=[vmem] * 2,
         out_shape=[
             jax.ShapeDtypeStruct((rows, width), jnp.bfloat16),
-            jax.ShapeDtypeStruct((rows * req_size, model), jnp.bfloat16),
+            jax.ShapeDtypeStruct((each, vocab * req_size * tp_size), jnp.float32),
         ],
         scratch_shapes=[
             pltpu.VMEM((tp_size, rows, chunk), jnp.bfloat16),
@@ -413,13 +464,18 @@
             pltpu.VMEM((tp_size, rows, width), jnp.bfloat16),
             pltpu.VMEM((tp_size, rows, width), jnp.bfloat16),
             pltpu.VMEM((req_size, 4, rows, width), jnp.bfloat16),
+            pltpu.VMEM((req_size * rows, model), jnp.bfloat16),
+            pltpu.VMEM(output_head.shape, jnp.bfloat16),
+            pltpu.VMEM((req_size, tp_size, each, vocab), jnp.bfloat16),
+            pltpu.VMEM((req_size, tp_size, each, vocab), jnp.bfloat16),
             dma(tp_size), dma(tp_size), dma(tp_size), dma(tp_size), dma(tp_size), dma(tp_size),
-            dma(req_size, 4), dma(req_size, 4),
+            dma(req_size, 4), dma(req_size, 4), dma(req_size, tp_size), dma(req_size, tp_size),
+            dma(1),
         ],
         compiler_params=pltpu.CompilerParams(
             collective_id=1, has_side_effects=True, vmem_limit_bytes=40 << 20
         ),
-    )(summed, stats, gated, mixer_gain[None], mamba_out, attention_out, residual, final_gain[None])
+    )(summed, stats, gated, mixer_gain[None], mamba_out, attention_out, residual, final_gain[None], output_head)
 
 
 def body(
@@ -467,17 +523,9 @@
     new_conv_state = swap(new_conv)
     new_coupling_state = swap(new_coup)
     new_scan_state = new_state.reshape(scan_state.shape)
-    new_residual, final_rows = joint(
-        summed, stats, gated, mixer_gain, mamba_out, attention_out, residual, final_gain
-    )
-    vocab_logits = jnp.dot(
-        final_rows,
-        output_head,
-        preferred_element_type=jnp.float32,
-    )
-    logits = lax.all_to_all(
-        vocab_logits.astype(jnp.bfloat16), ("req", "tp"), split_axis=0, concat_axis=1, tiled=True
-    ).astype(vocab_logits.dtype)
+    new_residual, logits = joint(
+        summed, stats, gated, mixer_gain, mamba_out, attention_out, residual, final_gain, output_head
+    )
     return (new_residual, logits, new_scan_state, new_conv_state, new_coupling_state, new_key_value)
 
 

time: 95.2 us -> 90.7 us (0.953)
  Pallas kernels: 44.7 us -> 70.7 us
  waiting for transfers between devices: 25.6 us -> 0 us
  local copies, waits for them, and re-layouts: 12.6 us -> 17.3 us
  starting transfers between devices: 4.21 us -> 0 us
  matrix products: 3.96 us -> 0.65 us
  other arithmetic: 2.79 us -> 0 us
    pallas_call x1, Pallas kernels: 23.9 us -> 49.8 us  [joint(): pl.pallas_call(functools.partial(joint_kernel, tp_size, req_size), in_spe...]
    all_to_all x1 -> x0, waiting for transfers between devices: 25.6 us -> none  [body(): lax.all_to_all(vocab_logits.astype(jnp.bfloat16), ('req', 'tp'), split_ax...]
    unnamed x45 -> x46, local copies, waits for them, and re-layouts: 11.1 us -> 15.8 us
    all_to_all x1 -> x0, starting transfers between devices: 4.21 us -> none  [body(): lax.all_to_all(vocab_logits.astype(jnp.bfloat16), ('req', 'tp'), split_ax...]
    dot_general x1 -> x0, matrix products: 3.3 us -> none  [body(): jnp.dot(final_rows, output_head, preferred_element_type=jnp.float32)]
    convert_element_type x1 -> x0, other arithmetic: 2.79 us -> none  [body(): logits = lax.all_to_all(vocab_logits.astype(jnp.bfloat16), ('req', 'tp'),...]
  transfers between devices with their start and end apart: 1 -> 0, of which waited for: 1 -> 0; matrix products, arithmetic and copies ran while one was open for 1% -> 0% of each run, Pallas kernels for 0% -> 0%
where the time goes in v3:
time: 90.7 us; the launch traced here: 89.4 us
  Pallas kernels  70.7 us (78%)
  local copies, waits for them, and re-layouts  17.3 us (19%)
    pallas_call x1, Pallas kernels, joint(): pl.pallas_call(functools.partial(joint_kernel, tp_size, req_size), in_spe...  49.8 us
    unnamed x46, local copies, waits for them, and re-layouts  15.8 us
    pallas_call x1, Pallas kernels, mixer(): pl.pallas_call(mixer_kernel, grid=(rows // BR,), in_specs=[smem, smem, ro...  14.6 us
    pallas_call x1, Pallas kernels, entry(): pl.pallas_call(functools.partial(entry_kernel, tp_size), in_specs=[smem]...  6.32 us

profile of v3, /device:TPU:0, one launch (start us, length us, event | category | flops | bytes accessed | tf_op | source)
XLA Modules:
  0.0 89.4 jit_solution(4245562060957332547)
XLA Ops:
  0.6 0.0 copy-start
  0.6 0.0 copy-start.16
  0.7 0.0 copy-start.19
  0.7 0.0 copy-start.18
  0.7 0.8 broadcast_in_dim.10.mixer_gain_ref
  1.5 0.0 copy-start.3
  1.5 1.5 %copy-done.3 = bf16[2048,384]{1,0:T(8,128)(2,1)S(1)} copy-done((bf16[2048,384]{1,0:T(8,128)(2,1)S(1)}, bf16[2048,384]{1,0:T(8,128)(2,1)}, u32[]{:S(2)}) %copy-start.3) | copy-done | bytes 1572888
  3.1 0.0 copy-start.6
  3.1 1.0 %copy-done.6 = bf16[2048,128]{1,0:T(8,128)(2,1)S(1)} copy-done((bf16[2048,128]{1,0:T(8,128)(2,1)S(1)}, bf16[2048,128]{1,0:T(8,128)(2,1)}, u32[]{:S(2)}) %copy-start.6) | copy-done | bytes 524312
  4.1 0.0 copy-start.7
  4.1 0.9 %copy-done.7 = bf16[32,2048]{1,0:T(8,128)(2,1)S(1)} copy-done((bf16[32,2048]{1,0:T(8,128)(2,1)S(1)}, bf16[32,2048]{1,0:T(8,128)(2,1)}, u32[]{:S(2)}) %copy-start.7) | copy-done | bytes 131096
  5.0 0.0 copy-start.10
  5.0 0.7 copy-done.10
  5.7 0.8 copy-done.13
  6.5 0.0 copy-start.14
  6.5 0.7 copy-done.14
  7.2 0.0 copy-start.17
  7.2 0.7 copy-done.17
  7.9 0.0 copy-start.20
  7.9 0.7 copy-done.20
  8.5 0.0 copy-start.21
  8.5 0.7 copy-done.21
  9.2 0.0 copy-start.9
  9.2 0.0 copy-start.11
  9.2 0.0 copy-start.12
  9.2 6.3 %shard_map.253 = (bf16[32,2048]{1,0:T(8,128)(2,1)S(1)}, bf16[32,128]{1,0:T(8,128)(2,1)S(1)}, bf16[32,1536]{1,0:T(8,128)(2,1)S(1)}, bf16[32,512]{1,0:T(8,128)(2,1...) custom-call(f32[6]{0:T(128)S(1)} %copy-done.20, f32[6]{0:T(128)S(1)} %copy-done.21, bf16[32,2048]{1,0:T(8,128)(2,1)S(1)} %copy-done.7, ...), custom_call_target="tpu_custom_call" | custom-call | tf_op jit(solution)/shard_map/pallas_call | solution.py:111
  15.5 0.6 slice.3
  16.1 0.0 copy-done
  16.1 0.7 fusion.5.projected_ref
  16.8 0.0 copy-done.16
  16.8 0.0 copy-done.19
  16.8 0.0 copy-done.18
  16.8 0.0 copy-done.9
  16.8 0.0 copy-done.11
  16.8 0.0 copy-done.12
  16.9 0.0 copy-start.2
  16.9 2.8 %copy-done.2 = bf16[32,6,64,256]{3,2,1,0:T(8,128)(2,1)S(1)} copy-done((bf16[32,6,64,256]{3,2,1,0:T(8,128)(2,1)S(1)}, bf16[32,6,64,256]{3,2,1,0:T(8,128)(2,1)}, u32[]{:S(2)}) %copy-start.2) | copy-done | bytes 6291480
  19.6 0.0 copy-start.4
  19.7 14.6 %shard_map.254 = (bf16[32,384,256]{2,1,0:T(8,128)(2,1)}, bf16[3,32,384]{2,1,0:T(8,128)(2,1)}, bf16[3,32,128]{2,1,0:T(8,128)(2,1)}, bf16[4,32,256]{2,1,0:T(8,128)...) custom-call(s32[32]{0:T(128)S(1)} %copy-done.18, f32[6]{0:T(128)S(1)} %copy-done.19, ...), custom_call_target="tpu_custom_call" | custom-call | tf_op jit(solution)/shard_map/pallas_call | solution.py:239
  34.2 0.0 copy-done.4
  34.2 0.0 copy-done.5
  34.2 0.0 copy-done.8
  34.2 0.0 copy-done.15
  34.3 0.0 copy-start.1
  34.3 3.4 %copy-done.1 = bf16[2048,2048]{1,0:T(8,128)(2,1)S(1)} copy-done((bf16[2048,2048]{1,0:T(8,128)(2,1)S(1)}, bf16[2048,2048]{1,0:T(8,128)(2,1)}, u32[]{:S(2)}) %copy-start.1) | copy-done | bytes 8388632
  37.6 49.8 %shard_map.255 = (bf16[32,512]{1,0:T(8,128)(2,1)S(1)}, f32[8,65536]{1,0:T(8,128)S(1)}) custom-call(bf16[4,32,256]{2,1,0:T(8,128)(2,1)S(1)} %get-tuple-element.26.summed_ref, f32[32,128]{1,0:T(8,128)S(1)} %get-tuple-element.27.stats_ref, f32[32,384]{1,0:T(8,128)S(1)} %get-tuple-element.28.gated_ref, f32[1,384]{1,0:T(1,128)S(1)} %broadcast_in_dim.10.mixer_gain_ref, ...), custom_call_target="tpu_custom_call" | custom-call | tf_op jit(solution)/shard_map/pallas_call | solution.py:453
  87.5 0.6 copy.37
  88.1 1.3 %copy.38 = f32[8,65536]{1,0:T(8,128)} copy(f32[8,65536]{1,0:T(8,128)S(1)} %get-tuple-element.41) | data formatting | bytes 4194304
  (4 shorter events, 0.0 us)
Async XLA Ops:
  0.6 15.5 %copy-start = (bf16[2048,2,384]{2,1,0:T(2,128)(2,1)S(1)}, bf16[2048,2,384]{2,1,0:T(2,128)(2,1)}, u32[]{:S(2)}) copy-start(bf16[2048,2,384]{2,1,0:T(2,128)(2,1)} %param.25) | copy-start | bytes 9437188
  0.6 16.2 %copy-start.16 = (bf16[4,384]{1,0:T(4,128)(2,1)S(1)}, bf16[4,384]{1,0:T(4,128)(2,1)}, u32[]{:S(2)}) copy-start(bf16[4,384]{1,0:T(4,128)(2,1)} %taps_ref.3) | copy-start | bytes 9220
  0.7 16.2 %copy-start.19 = (f32[6]{0:T(128)S(1)}, f32[6]{0:T(128)}, u32[]{:S(2)}) copy-start(f32[6]{0:T(128)} %skip_ref.1) | copy-start | bytes 76
  0.7 16.2 %copy-start.18 = (s32[32]{0:T(128)S(1)}, s32[32]{0:T(128)}, u32[]{:S(2)}) copy-start(s32[32]{0:T(128)} %len_ref.1) | copy-start | bytes 388
  1.5 1.5 %copy-start.3 = (bf16[2048,384]{1,0:T(8,128)(2,1)S(1)}, bf16[2048,384]{1,0:T(8,128)(2,1)}, u32[]{:S(2)}) copy-start(bf16[2048,384]{1,0:T(8,128)(2,1)} %attention_ref.1) | copy-start | bytes 4718596
  3.1 1.0 %copy-start.6 = (bf16[2048,128]{1,0:T(8,128)(2,1)S(1)}, bf16[2048,128]{1,0:T(8,128)(2,1)}, u32[]{:S(2)}) copy-start(bf16[2048,128]{1,0:T(8,128)(2,1)} %coupling_ref.1) | copy-start | bytes 1572868
  4.1 0.9 %copy-start.7 = (bf16[32,2048]{1,0:T(8,128)(2,1)S(1)}, bf16[32,2048]{1,0:T(8,128)(2,1)}, u32[]{:S(2)}) copy-start(bf16[32,2048]{1,0:T(8,128)(2,1)} %residual_ref.3) | copy-start | bytes 393220
  5.0 0.7 copy-start.10
  5.7 0.8 copy-start.13
  6.5 0.7 copy-start.14
  7.2 0.7 copy-start.17
  7.9 0.7 copy-start.20
  8.5 0.7 copy-start.21
  9.2 7.6 %copy-start.9 = (bf16[32,4,512]{2,1,0:T(4,128)(2,1)S(1)}, bf16[32,4,512]{2,1,0:T(4,128)(2,1)}, u32[]{:S(2)}) copy-start(bf16[32,4,512]{2,1,0:T(4,128)(2,1)} %sink_ref.1) | copy-start | bytes 393220
  9.2 7.7 %copy-start.11 = (bf16[32,3,128]{2,0,1:T(8,128)(2,1)S(1)}, bf16[32,3,128]{2,0,1:T(8,128)(2,1)}, u32[]{:S(2)}) copy-start(bf16[32,3,128]{2,0,1:T(8,128)(2,1)} %param.34) | copy-start | bytes 73732
  9.2 7.7 %copy-start.12 = (bf16[32,3,384]{2,0,1:T(8,128)(2,1)S(1)}, bf16[32,3,384]{2,0,1:T(8,128)(2,1)}, u32[]{:S(2)}) copy-start(bf16[32,3,384]{2,0,1:T(8,128)(2,1)} %param.31) | copy-start | bytes 221188
  16.9 2.8 %copy-start.2 = (bf16[32,6,64,256]{3,2,1,0:T(8,128)(2,1)S(1)}, bf16[32,6,64,256]{3,2,1,0:T(8,128)(2,1)}, u32[]{:S(2)}) copy-start(bf16[32,6,64,256]{3,2,1,0:T(8,128)(2,1)} %param.35) | copy-start | bytes 18874372
  19.6 14.6 %copy-start.4 = (bf16[384,2048]{1,0:T(8,128)(2,1)S(1)}, bf16[384,2048]{1,0:T(8,128)(2,1)}, u32[]{:S(2)}) copy-start(bf16[384,2048]{1,0:T(8,128)(2,1)} %mamba_out_ref.1) | copy-start | bytes 4718596
  19.6 14.6 %copy-start.5 = (bf16[256,2048]{1,0:T(8,128)(2,1)S(1)}, bf16[256,2048]{1,0:T(8,128)(2,1)}, u32[]{:S(2)}) copy-start(bf16[256,2048]{1,0:T(8,128)(2,1)} %attention_out_ref.1) | copy-start | bytes 3145732
  19.7 14.6 %copy-start.8 = (bf16[32,2048]{1,0:T(8,128)(2,1)S(1)}, bf16[32,2048]{1,0:T(8,128)(2,1)}, u32[]{:S(2)}) copy-start(bf16[32,2048]{1,0:T(8,128)(2,1)} %residual_ref.3) | copy-start | bytes 393220
  19.7 14.6 %copy-start.15 = (f32[2048]{0:T(1024)S(1)}, f32[2048]{0:T(1024)}, u32[]{:S(2)}) copy-start(f32[2048]{0:T(1024)} %param.42) | copy-start | bytes 24580
  34.3 3.4 %copy-start.1 = (bf16[2048,2048]{1,0:T(8,128)(2,1)S(1)}, bf16[2048,2048]{1,0:T(8,128)(2,1)}, u32[]{:S(2)}) copy-start(bf16[2048,2048]{1,0:T(8,128)(2,1)} %head_ref.1) | copy-start | bytes 25165828

commit v4 on v3

--- a/solution.py
+++ b/solution.py
@@ -122,7 +122,7 @@
         ],
         scratch_shapes=[dma] * 4,
         compiler_params=pltpu.CompilerParams(
-            collective_id=0, has_side_effects=True, vmem_limit_bytes=16 << 20
+            collective_id=0, has_side_effects=True, vmem_limit_bytes=60 << 20
         ),
     )(bias, decay_log, residual, gain[None], attention_weight, coupling_weight, taps, state, step_weight)
 
@@ -261,7 +261,7 @@
             pltpu.VMEM((BR * QH, HD), jnp.float32),
             pltpu.VMEM((BR, EXTRA, 2 * KVH * HD), jnp.float32),
         ],
-        compiler_params=pltpu.CompilerParams(vmem_limit_bytes=40 << 20),
+        compiler_params=pltpu.CompilerParams(vmem_limit_bytes=60 << 20),
     )(
         lengths, skip, qkv, sink, window, state, coup, pre, coup_state, projected, taps, conv_state,
         step, decay,
@@ -473,7 +473,7 @@
             dma(1),
         ],
         compiler_params=pltpu.CompilerParams(
-            collective_id=1, has_side_effects=True, vmem_limit_bytes=40 << 20
+            collective_id=1, has_side_effects=True, vmem_limit_bytes=60 << 20
         ),
     )(summed, stats, gated, mixer_gain[None], mamba_out, attention_out, residual, final_gain[None], output_head)
 

time: 90.7 us -> 87 us (0.959)
  local copies, waits for them, and re-layouts: 17.3 us -> 7.22 us
  Pallas kernels: 70.7 us -> 75.7 us
  matrix products: 0.65 us -> 2.17 us
    unnamed x46 -> x4, local copies, waits for them, and re-layouts: 15.8 us -> 4.43 us
    pallas_call x1, Pallas kernels: 49.8 us -> 52.3 us  [joint(): pl.pallas_call(functools.partial(joint_kernel, tp_size, req_size), in_spe...]
    pallas_call x1, Pallas kernels: 6.32 us -> 8.18 us  [entry(): pl.pallas_call(functools.partial(entry_kernel, tp_size), in_specs=[smem]...]
    dot_general x1, matrix products: 0.65 us -> 2.17 us  [body(): jnp.einsum('rd,dtc->trc', normed, inner_weight, preferred_element_type=jn...]
where the time goes in v4:
time: 87 us; the launch traced here: 85.8 us
  Pallas kernels  75.7 us (87%)
  local copies, waits for them, and re-layouts  7.22 us (8%)
  matrix products  2.17 us (2%)
    pallas_call x1, Pallas kernels, joint(): pl.pallas_call(functools.partial(joint_kernel, tp_size, req_size), in_spe...  52.3 us
    pallas_call x1, Pallas kernels, mixer(): pl.pallas_call(mixer_kernel, grid=(rows // BR,), in_specs=[smem, smem, ro...  15.2 us
    pallas_call x1, Pallas kernels, entry(): pl.pallas_call(functools.partial(entry_kernel, tp_size), in_specs=[smem]...  8.18 us
    unnamed x4, local copies, waits for them, and re-layouts  4.43 us
    dot_general x1, matrix products, body(): jnp.einsum('rd,dtc->trc', normed, inner_weight, preferred_element_type=jn...  2.17 us

profile of v4, /device:TPU:0, one launch (start us, length us, event | category | flops | bytes accessed | tf_op | source)
XLA Modules:
  0.0 85.8 jit_solution(15766296909528933801)
XLA Ops:
  0.6 0.0 copy-start
  0.6 1.4 %broadcast_in_dim.10.mixer_gain_ref = f32[1,384]{1,0:T(1,128)} reshape(f32[384]{0:T(512)} %param.36) | data formatting | bytes 3072 | tf_op jit(solution)/shard_map/broadcast_in_dim | solution.py:478
  2.1 8.2 %shard_map.253 = (bf16[32,2048]{1,0:T(8,128)(2,1)}, bf16[32,128]{1,0:T(8,128)(2,1)}, bf16[32,1536]{1,0:T(8,128)(2,1)}, bf16[32,512]{1,0:T(8,128)(2,1)}, f32[32,384]{1,0:T(8,128)}, /*index=5*/f32[32,384]{1,0:T(8,128)}) custom-call(f32[6]{0:T(128)} %bias_ref.1, f32[6]{0:T(128)} %log_ref.1, bf16[32,2048]{1,0:T(8,128)(2,1)} %residual_ref.3, f32[1,2048]{1,0:T(1,128)} %bitcast.19, ...), custom_call_target="tpu_custom_call" | custom-call | tf_op jit(solution)/shard_map/pallas_call | solution.py:111
  10.2 1.4 %slice.3 = bf16[32,512]{1,0:T(8,128)(2,1)} slice(bf16[32,1536]{1,0:T(8,128)(2,1)} %get-tuple-element.20.qkv_ref), slice={[0:32], [1024:1536]} | slice | bytes 65536 | tf_op jit(solution)/shard_map/slice | solution.py:517
  11.6 0.0 copy-done
  11.6 2.2 %fusion.5.projected_ref = bf16[2,32,384]{2,1,0:T(8,128)(2,1)} fusion(bf16[2048,2,384]{2,1,0:T(2,128)(2,1)S(1)} %copy-done, bf16[32,2048]{1,0:T(8,128)(2,1)} %get-tuple-element.23), kind=kOutput, calls=%fused_computation.3 | convolution fusion | flops 100687872 | bytes 3325952 | tf_op jit(solution)/shard_map/rd,dtc->trc/dot_general | solution.py:514
  13.8 15.2 %shard_map.254 = (bf16[32,384,256]{2,1,0:T(8,128)(2,1)}, bf16[3,32,384]{2,1,0:T(8,128)(2,1)}, bf16[3,32,128]{2,1,0:T(8,128)(2,1)}, bf16[4,32,256]{2,1,0:T(8,128)...) custom-call(s32[32]{0:T(128)} %len_ref.1, f32[6]{0:T(128)} %skip_ref.1, bf16[32,1536]{1,0:T(8,128)(2,1)} %get-tuple-element.20.qkv_ref, ...), custom_call_target="tpu_custom_call" | custom-call | tf_op jit(solution)/shard_map/pallas_call | solution.py:239
  29.0 52.3 %shard_map.255 = (bf16[32,512]{1,0:T(8,128)(2,1)}, f32[8,65536]{1,0:T(8,128)}) custom-call(bf16[4,32,256]{2,1,0:T(8,128)(2,1)} %get-tuple-element.26.summed_ref, f32[32,128]{1,0:T(8,128)} %get-tuple-element.27.stats_ref, f32[32,384]{1,0:T(8,128)} %get-tuple-element.28.gated_ref, f32[1,384]{1,0:T(1,128)} %broadcast_in_dim.10.mixer_gain_ref, ...), custom_call_target="tpu_custom_call" | custom-call | tf_op jit(solution)/shard_map/pallas_call | solution.py:453
  81.4 1.4 %copy.37 = bf16[32,512]{1,0:T(8,128)(2,1)} copy(bf16[32,512]{1,0:T(8,128)(2,1)} %get-tuple-element.40) | data formatting | bytes 65536
  82.7 3.0 %copy.38 = f32[8,65536]{1,0:T(8,128)} copy(f32[8,65536]{1,0:T(8,128)} %get-tuple-element.41) | data formatting | bytes 4194304
Async XLA Ops:
  0.6 11.0 %copy-start = (bf16[2048,2,384]{2,1,0:T(2,128)(2,1)S(1)}, bf16[2048,2,384]{2,1,0:T(2,128)(2,1)}, u32[]{:S(2)}) copy-start(bf16[2048,2,384]{2,1,0:T(2,128)(2,1)} %param.25) | copy-start | bytes 9437188
